TPU v7x, 32 devices: a whole 2x2x4 slice. The times are simulated.
32 devices in a mesh: outer: 4 (over y, x), inner: 8 (over z, core).
Axes of the slice: x: 2, y: 2, z: 4, core: 2. Of those that a mesh axis runs over, the one named last changes fastest.
Arguments:
- queries: bfloat16 [4096, 2048], P(('outer', 'inner')), may hold values from -6 to 6
- key_rows: bfloat16 [4096, 2048], P(('outer', 'inner')), may hold values from -6 to 6
- value_rows: bfloat16 [4096, 2048], P(('outer', 'inner')), may hold values from -6 to 6
- beta_logit: bfloat16 [4096, 16], P(('outer', 'inner')), may hold values from -8 to 2, as said below
- log_gate: bfloat16 [4096, 16], P(('outer', 'inner')), may hold values from -1 to 0, as said below
- out_grad: bfloat16 [4096, 2048], P(('outer', 'inner')), may hold values from -6 to 6
- block_states: float32 [4, 16, 128, 128], P('outer', 'inner'), may hold values from -4 to 4
Outputs:
- query_gradient: bfloat16 [4096, 2048], P(('outer', 'inner'))
- grad_keys: bfloat16 [4096, 2048], P(('outer', 'inner'))
- grad_values: bfloat16 [4096, 2048], P(('outer', 'inner'))
- grad_beta: bfloat16 [4096, 16], P(('outer', 'inner'))
- grad_gate: bfloat16 [4096, 16], P(('outer', 'inner'))
Inputs may be any that keep to these rules, and one draw needn't show every extreme that they name: `beta_logit`: within each head the logits lie within 1 of a level drawn for each head. `log_gate`: negative in every entry.
All inputs are finite; a program needn't handle non-finite values.
Results may differ from a plain program's by a relative error of at most 0.002.
Values may be sent and summed in bfloat16 or wider, within the bound.
A program may use at most 128 MiB of HBM per device.

v0:
```python
import jax
import jax.numpy as jnp
from jax import lax
from jax.sharding import PartitionSpec as P

DK = 128
DV = 128
GROUP = 128


precise = lax.Precision.HIGHEST


def unit_rows(matrix):
    return matrix * lax.rsqrt(jnp.sum(matrix * matrix, axis=-1, keepdims=True) + 1e-06)


def group_step(carried, inputs):
    state_now, transition, grad_sum = carried
    query_part, key_part, value_part, strength, gate_part, cotangent_part = inputs
    group_len = query_part.shape[1]
    key_width = key_part.shape[2]
    row_index = jnp.arange(group_len)[:, None]
    col_index = jnp.arange(group_len)[None, :]
    inclusive = row_index >= col_index
    strictly_lower = row_index > col_index
    cumulative = jnp.cumsum(gate_part, axis=1)
    gaps = cumulative[:, :, None] - cumulative[:, None, :]
    decay_mat = jnp.where(inclusive, jnp.exp(jnp.where(inclusive, gaps, 0.0)), 0.0)
    key_gram = jnp.einsum("hid,hjd->hij", key_part, key_part, precision=precise)
    lower_mat = strength[:, :, None] * jnp.where(strictly_lower, decay_mat, 0.0) * key_gram
    unit_lower = lower_mat + jnp.eye(group_len, dtype=jnp.float32)
    growth = jnp.exp(cumulative)
    right_side = jnp.concatenate(
        [(strength * growth)[:, :, None] * key_part, strength[:, :, None] * value_part], axis=2
    )
    solution_matrix = lax.linalg.triangular_solve(
        unit_lower, right_side, left_side=True, lower=True, unit_diagonal=True
    )
    write_keys = solution_matrix[:, :, :key_width]
    write_values = solution_matrix[:, :, key_width:]
    new_values = write_values - jnp.einsum("hcd,hde->hce", write_keys, state_now, precision=precise)
    scores = jnp.einsum("hid,hjd->hij", query_part, key_part, precision=precise) * decay_mat
    grown_queries = query_part * growth[:, :, None]
    output = jnp.einsum("hcd,hde->hce", grown_queries, state_now, precision=precise)
    output = output + jnp.einsum("hij,hje->hie", scores, new_values, precision=precise)
    tail_decay = jnp.exp(cumulative[:, -1:] - cumulative)
    tail_keys = key_part * tail_decay[:, :, None]
    last_growth = growth[:, -1][:, None, None]
    state_next = last_growth * state_now + jnp.einsum(
        "hcd,hce->hde", tail_keys, new_values, precision=precise
    )
    detached = lax.stop_gradient
    state_queries = detached(
        grown_queries - jnp.einsum("hij,hjd->hid", scores, write_keys, precision=precise)
    )
    projected = jnp.einsum("hcd,hce->hde", state_queries, cotangent_part, precision=precise)
    grad_sum = grad_sum + jnp.einsum("hji,hje->hie", transition, projected, precision=precise)
    step_trans = detached(
        last_growth * jnp.eye(key_width, dtype=jnp.float32)
        - jnp.einsum("hcd,hce->hde", tail_keys, write_keys, precision=precise)
    )
    transition = jnp.einsum("hij,hjk->hik", step_trans, transition, precision=precise)
    return ((state_next, transition, grad_sum), output)


def block_forward(queries, keys_in, values, logits, gates, start_state, cotangent, group_size):
    head_count, length, key_width = queries.shape
    group_count = length // group_size

    def to_groups(array_in):
        shaped = array_in.reshape((head_count, group_count, group_size) + array_in.shape[2:])
        return jnp.moveaxis(shaped, 1, 0)

    inputs = (
        to_groups(unit_rows(queries)),
        to_groups(unit_rows(keys_in)),
        to_groups(values),
        to_groups(jax.nn.sigmoid(logits)),
        to_groups(gates),
        to_groups(cotangent),
    )
    identity = jnp.broadcast_to(
        jnp.eye(key_width, dtype=jnp.float32), (head_count, key_width, key_width)
    )
    grad_zero = jnp.zeros(start_state.shape, jnp.float32)
    (final_state, transition, grad_sum), outputs = lax.scan(
        group_step, (start_state, identity, grad_zero), inputs
    )
    outputs = jnp.moveaxis(outputs, 0, 1).reshape(head_count, length, -1)
    return ((outputs, final_state), (transition, grad_sum))


def matmul_heads(left_mat, right_mat):
    return jnp.einsum("hij,hjk->hik", left_mat, right_mat, precision=precise)


def head_split(array_in, width):
    return array_in.astype(jnp.float32).reshape(array_in.shape[0], -1, width).transpose(1, 0, 2)


def merge_heads(array_in):
    return array_in.transpose(1, 0, 2).reshape(array_in.shape[1], -1).astype(jnp.bfloat16)


def prepare(queries, key_rows, value_rows, out_grad, beta_logit, log_gate):
    return (
        head_split(queries, DK),
        head_split(key_rows, DK),
        head_split(value_rows, DV),
        beta_logit.astype(jnp.float32).T,
        log_gate.astype(jnp.float32).T,
        head_split(out_grad, DV),
    )


def block_pullback(pieces, start_state):
    query_in, key_in, value_in, logit_in, gate_in, cotangent = pieces

    def forward(query_arg, key_arg, value_arg, logit_arg, gate_arg, state_arg):
        return block_forward(
            query_arg, key_arg, value_arg, logit_arg, gate_arg, state_arg, cotangent, GROUP
        )

    unused_out, pull_back, side = jax.vjp(
        forward, query_in, key_in, value_in, logit_in, gate_in, start_state, has_aux=True
    )
    turned = jnp.swapaxes(side[0], 1, 2)

    def finish(incoming):
        gradients = pull_back((cotangent, incoming))
        return gradients[:5]

    return (turned, side[1], finish)


def fold_later(matrices, state_grads, position):
    total_blocks = matrices.shape[0]

    def advance(turn_index, running):
        block_index = total_blocks - 1 - turn_index
        updated = matmul_heads(matrices[block_index], running) + state_grads[block_index]
        return jnp.where(block_index > position, updated, running)

    return lax.fori_loop(0, total_blocks, advance, jnp.zeros_like(state_grads[0]))


def shards(queries, key_rows, value_rows, beta_logit, log_gate, out_grad, block_states):
    arrived = (
        lax.all_to_all(queries, "inner", split_axis=1, concat_axis=0, tiled=True),
        lax.all_to_all(key_rows, "inner", split_axis=1, concat_axis=0, tiled=True),
        lax.all_to_all(value_rows, "inner", split_axis=1, concat_axis=0, tiled=True),
        lax.all_to_all(out_grad, "inner", split_axis=1, concat_axis=0, tiled=True),
        lax.all_to_all(beta_logit, "inner", split_axis=1, concat_axis=0, tiled=True),
        lax.all_to_all(log_gate, "inner", split_axis=1, concat_axis=0, tiled=True),
    )
    pieces = prepare(arrived[0], arrived[1], arrived[2], arrived[3], arrived[4], arrived[5])
    start_state = block_states[0]
    turned, grad_start, finish = block_pullback(pieces, start_state)
    gathered = (
        lax.all_gather(turned[None], "outer", axis=0, tiled=True),
        lax.all_gather(grad_start[None], "outer", axis=0, tiled=True),
    )
    incoming = fold_later(gathered[0], gathered[1], lax.axis_index("outer"))
    gradients = finish(incoming)
    result = (
        lax.all_to_all(merge_heads(gradients[0]), "inner", split_axis=0, concat_axis=1, tiled=True),
        lax.all_to_all(merge_heads(gradients[1]), "inner", split_axis=0, concat_axis=1, tiled=True),
        lax.all_to_all(merge_heads(gradients[2]), "inner", split_axis=0, concat_axis=1, tiled=True),
        lax.all_to_all(
            gradients[3].T.astype(jnp.bfloat16), "inner", split_axis=0, concat_axis=1, tiled=True
        ),
        lax.all_to_all(
            gradients[4].T.astype(jnp.bfloat16), "inner", split_axis=0, concat_axis=1, tiled=True
        ),
    )
    return (result[0], result[1], result[2], result[3], result[4])


def solution(mesh):
    return jax.shard_map(
        shards,
        mesh=mesh,
        in_specs=(
            P(("outer", "inner"), None),
            P(("outer", "inner"), None),
            P(("outer", "inner"), None),
            P(("outer", "inner"), None),
            P(("outer", "inner"), None),
            P(("outer", "inner"), None),
            P("outer", "inner", None, None),
        ),
        out_specs=(
            P(("outer", "inner"), None),
            P(("outer", "inner"), None),
            P(("outer", "inner"), None),
            P(("outer", "inner"), None),
            P(("outer", "inner"), None),
        ),
        check_vma=False,
    )
```

profile of v0, /device:TPU:25, one launch (start us, length us, event | category | flops | bytes accessed | tf_op | source)
XLA Modules:
  0.0 871.0 jit_solution(8195031747380546615)
XLA Ops:
  0.6 7.4 all_to_all.164
  8.1 6.8 all-to-all-start
  17.0 6.9 all-to-all-start.1
  25.0 11.7 %all-to-all-done.1 = bf16[128,8,256]{0,2,1:T(8,128)(2,1)S(1)} async-done(((bf16[128,8,256]{0,2,1:T(8,128)(2,1)}), bf16[128,8,256]{0,2,1:T(8,128)(2,1)S(1)}, u32[]{:S(2)}, u32[]{:S(2)}) %all-to-all-start.1) | async-done | bytes 524320 | tf_op jit(solution)/shard_map/all_to_all | solution.py:151
  46.6 8.8 %all-to-all-done.4 = bf16[128,8,256]{0,2,1:T(8,128)(2,1)S(1)} async-done(((bf16[128,8,256]{0,2,1:T(8,128)(2,1)}), bf16[128,8,256]{0,2,1:T(8,128)(2,1)S(1)}, u32[]{:S(2)}, u32[]{:S(2)}) %all-to-all-start.4) | async-done | bytes 524320 | tf_op jit(solution)/shard_map/all_to_all | solution.py:150
  55.4 6.7 all-to-all-start.3
  63.4 11.6 %all-to-all-done.3 = bf16[128,8,256]{0,2,1:T(8,128)(2,1)} async-done(((bf16[128,8,256]{0,2,1:T(8,128)(2,1)}), bf16[128,8,256]{0,2,1:T(8,128)(2,1)}, u32[]{:S(2)}, u32[]{:S(2)}) %all-to-all-start.3) | async-done | bytes 524320 | tf_op jit(solution)/shard_map/all_to_all | solution.py:152
  112.4 269.3 %while.108 = (s32[]{:T(128)}, f32[2,128,128]{2,1,0:T(8,128)S(1)}, f32[2,128,128]{2,1,0:T(8,128)S(1)}, f32[2,128,128]{1,2,0:T(8,128)S(1)}, f32[8,2,128,128]{3,2,1...) while((s32[]{:T(128)}, f32[2,128,128]{2,1,0:T(8,128)S(1)}, ...), condition=%wide.region_4.5_spmd.clone.clone, body=%wide.region_2.4_spmd.clone.clone.sunk | while | flops 555172992 | bytes 8843675 | solution.py:87
  116.8 19.7 %custom-call.48 = f32[2,1,128,128]{2,3,1,0:T(8,128)S(1)} custom-call(f32[2,1,128,128]{3,2,1,0:T(8,128)S(1)} %get-tuple-element.3072), custom_call_target="InvertDiagBlocksLowerTriangular" | custom-call | tf_op jit(solution)/shard_map/jvp()/while/body/eval_jaxpr/triangular_solve | solution.py:37
  150.4 19.7 %custom-call.48 = f32[2,1,128,128]{2,3,1,0:T(8,128)S(1)} custom-call(f32[2,1,128,128]{3,2,1,0:T(8,128)S(1)} %get-tuple-element.3072), custom_call_target="InvertDiagBlocksLowerTriangular" | custom-call | tf_op jit(solution)/shard_map/jvp()/while/body/eval_jaxpr/triangular_solve | solution.py:37
  184.1 19.7 %custom-call.48 = f32[2,1,128,128]{2,3,1,0:T(8,128)S(1)} custom-call(f32[2,1,128,128]{3,2,1,0:T(8,128)S(1)} %get-tuple-element.3072), custom_call_target="InvertDiagBlocksLowerTriangular" | custom-call | tf_op jit(solution)/shard_map/jvp()/while/body/eval_jaxpr/triangular_solve | solution.py:37
  217.8 19.7 %custom-call.48 = f32[2,1,128,128]{2,3,1,0:T(8,128)S(1)} custom-call(f32[2,1,128,128]{3,2,1,0:T(8,128)S(1)} %get-tuple-element.3072), custom_call_target="InvertDiagBlocksLowerTriangular" | custom-call | tf_op jit(solution)/shard_map/jvp()/while/body/eval_jaxpr/triangular_solve | solution.py:37
  251.4 19.7 %custom-call.48 = f32[2,1,128,128]{2,3,1,0:T(8,128)S(1)} custom-call(f32[2,1,128,128]{3,2,1,0:T(8,128)S(1)} %get-tuple-element.3072), custom_call_target="InvertDiagBlocksLowerTriangular" | custom-call | tf_op jit(solution)/shard_map/jvp()/while/body/eval_jaxpr/triangular_solve | solution.py:37
  285.1 19.7 %custom-call.48 = f32[2,1,128,128]{2,3,1,0:T(8,128)S(1)} custom-call(f32[2,1,128,128]{3,2,1,0:T(8,128)S(1)} %get-tuple-element.3072), custom_call_target="InvertDiagBlocksLowerTriangular" | custom-call | tf_op jit(solution)/shard_map/jvp()/while/body/eval_jaxpr/triangular_solve | solution.py:37
  318.7 19.7 %custom-call.48 = f32[2,1,128,128]{2,3,1,0:T(8,128)S(1)} custom-call(f32[2,1,128,128]{3,2,1,0:T(8,128)S(1)} %get-tuple-element.3072), custom_call_target="InvertDiagBlocksLowerTriangular" | custom-call | tf_op jit(solution)/shard_map/jvp()/while/body/eval_jaxpr/triangular_solve | solution.py:37
  352.3 19.7 %custom-call.48 = f32[2,1,128,128]{2,3,1,0:T(8,128)S(1)} custom-call(f32[2,1,128,128]{3,2,1,0:T(8,128)S(1)} %get-tuple-element.3072), custom_call_target="InvertDiagBlocksLowerTriangular" | custom-call | tf_op jit(solution)/shard_map/jvp()/while/body/eval_jaxpr/triangular_solve | solution.py:37
  381.8 10.2 %all-gather = f32[8,128,128]{2,1,0:T(8,128)} all-gather(f32[2,128,128]{2,1,0:T(8,128)S(1)} %bitcast.630), channel_id=2, replica_groups=mesh['outer'=4,'inner'=8] {'outer'}, dimensions={0}, use_global_device_ids=true | all-gather | bytes 655360 | tf_op jit(solution)/shard_map/all_gather | solution.py:161
  392.1 8.3 all-gather.1
  407.7 380.4 %while.106 = (s32[]{:T(128)}, f32[2,128,128]{2,1,0:T(8,128)S(1)}, f32[8,2,128,128]{3,2,0,1:T(8,128)}, f32[8,2,128,128]{3,2,0,1:T(8,128)}, bf16[8,2,128,128]{3,2,...) while((s32[]{:T(128)}, f32[2,128,128]{2,1,0:T(8,128)S(1)}, ...), condition=%wide.region_18.19_spmd.clone.clone, body=%wide.region_7.18_spmd.clone.clone.sunk | while | flops 857327744 | bytes 11667445 | solution.py:87
  412.6 19.7 %custom-call.47 = f32[2,1,128,128]{2,3,1,0:T(8,128)S(1)} custom-call(f32[2,1,128,128]{3,2,1,0:T(8,128)S(1)} %add_bitcast_fusion.4), custom_call_target="InvertDiagBlocksLowerTriangular" | custom-call | tf_op jit(solution)/shard_map/transpose(jvp())/while/body/eval_jaxpr/triangular_solve | solution.py:37
  460.1 19.7 %custom-call.47 = f32[2,1,128,128]{2,3,1,0:T(8,128)S(1)} custom-call(f32[2,1,128,128]{3,2,1,0:T(8,128)S(1)} %add_bitcast_fusion.4), custom_call_target="InvertDiagBlocksLowerTriangular" | custom-call | tf_op jit(solution)/shard_map/transpose(jvp())/while/body/eval_jaxpr/triangular_solve | solution.py:37
  507.7 19.7 %custom-call.47 = f32[2,1,128,128]{2,3,1,0:T(8,128)S(1)} custom-call(f32[2,1,128,128]{3,2,1,0:T(8,128)S(1)} %add_bitcast_fusion.4), custom_call_target="InvertDiagBlocksLowerTriangular" | custom-call | tf_op jit(solution)/shard_map/transpose(jvp())/while/body/eval_jaxpr/triangular_solve | solution.py:37
  555.3 19.7 %custom-call.47 = f32[2,1,128,128]{2,3,1,0:T(8,128)S(1)} custom-call(f32[2,1,128,128]{3,2,1,0:T(8,128)S(1)} %add_bitcast_fusion.4), custom_call_target="InvertDiagBlocksLowerTriangular" | custom-call | tf_op jit(solution)/shard_map/transpose(jvp())/while/body/eval_jaxpr/triangular_solve | solution.py:37
  602.8 19.7 %custom-call.47 = f32[2,1,128,128]{2,3,1,0:T(8,128)S(1)} custom-call(f32[2,1,128,128]{3,2,1,0:T(8,128)S(1)} %add_bitcast_fusion.4), custom_call_target="InvertDiagBlocksLowerTriangular" | custom-call | tf_op jit(solution)/shard_map/transpose(jvp())/while/body/eval_jaxpr/triangular_solve | solution.py:37
  650.4 19.7 %custom-call.47 = f32[2,1,128,128]{2,3,1,0:T(8,128)S(1)} custom-call(f32[2,1,128,128]{3,2,1,0:T(8,128)S(1)} %add_bitcast_fusion.4), custom_call_target="InvertDiagBlocksLowerTriangular" | custom-call | tf_op jit(solution)/shard_map/transpose(jvp())/while/body/eval_jaxpr/triangular_solve | solution.py:37
  697.9 19.7 %custom-call.47 = f32[2,1,128,128]{2,3,1,0:T(8,128)S(1)} custom-call(f32[2,1,128,128]{3,2,1,0:T(8,128)S(1)} %add_bitcast_fusion.4), custom_call_target="InvertDiagBlocksLowerTriangular" | custom-call | tf_op jit(solution)/shard_map/transpose(jvp())/while/body/eval_jaxpr/triangular_solve | solution.py:37
  745.5 19.7 %custom-call.47 = f32[2,1,128,128]{2,3,1,0:T(8,128)S(1)} custom-call(f32[2,1,128,128]{3,2,1,0:T(8,128)S(1)} %add_bitcast_fusion.4), custom_call_target="InvertDiagBlocksLowerTriangular" | custom-call | tf_op jit(solution)/shard_map/transpose(jvp())/while/body/eval_jaxpr/triangular_solve | solution.py:37
  792.7 8.2 all-to-all-start.9
  802.8 6.8 all-to-all-start.10
  821.5 9.7 %all-to-all-done.7 = bf16[8,128,256]{1,2,0:T(8,128)(2,1)S(1)} async-done(((bf16[8,128,256]{1,2,0:T(8,128)(2,1)}), bf16[8,128,256]{1,2,0:T(8,128)(2,1)S(1)}, u32[]{:S(2)}, u32[]{:S(2)}) %all-to-all-start.7) | async-done | bytes 524320 | tf_op jit(solution)/shard_map/all_to_all | solution.py:168
  838.5 11.5 %all-to-all-done.6 = bf16[8,128,256]{1,2,0:T(8,128)(2,1)S(1)} async-done(((bf16[8,128,256]{1,2,0:T(8,128)(2,1)}), bf16[8,128,256]{1,2,0:T(8,128)(2,1)S(1)}, u32[]{:S(2)}, u32[]{:S(2)}) %all-to-all-start.6) | async-done | bytes 524320 | tf_op jit(solution)/shard_map/all_to_all | solution.py:167
  858.1 10.7 %all-to-all-done.8 = bf16[8,128,256]{1,2,0:T(8,128)(2,1)S(1)} async-done(((bf16[8,128,256]{1,2,0:T(8,128)(2,1)}), bf16[8,128,256]{1,2,0:T(8,128)(2,1)S(1)}, u32[]{:S(2)}, u32[]{:S(2)}) %all-to-all-start.8) | async-done | bytes 524320 | tf_op jit(solution)/shard_map/all_to_all | solution.py:169
  (629 shorter events, 432.4 us)
Async XLA Ops:
  0.6 23.3 %copy-start.5 = (bf16[128,2048]{1,0:T(8,128)(2,1)S(1)}, bf16[128,2048]{1,0:T(8,128)(2,1)}, u32[]{:S(2)}) copy-start(bf16[128,2048]{1,0:T(8,128)(2,1)} %param.13) | copy-start | bytes 1572868
  8.1 8.9 %all-to-all-start = ((bf16[128,8,2]{0,2,1:T(2,128)(2,1)}), bf16[128,8,2]{0,2,1:T(2,128)(2,1)S(1)}, u32[]{:S(2)}, u32[]{:S(2)}) async-start(bf16[128,8,2]{0,2,1:T(2,128)(2,1)} %bitcast.639), calls=%async_computation | async-start | bytes 8192 | tf_op jit(solution)/shard_map/all_to_all | solution.py:155
  14.9 28.0 %copy-start.6 = (bf16[128,2048]{1,0:T(8,128)(2,1)S(1)}, bf16[128,2048]{1,0:T(8,128)(2,1)}, u32[]{:S(2)}) copy-start(bf16[128,2048]{1,0:T(8,128)(2,1)} %param.15) | copy-start | bytes 1572868
  17.0 26.9 %copy-start.7 = (bf16[128,2048]{1,0:T(8,128)(2,1)S(1)}, bf16[128,2048]{1,0:T(8,128)(2,1)}, u32[]{:S(2)}) copy-start(bf16[128,2048]{1,0:T(8,128)(2,1)} %param.18) | copy-start | bytes 1572868
  17.0 19.6 %all-to-all-start.1 = ((bf16[128,8,256]{0,2,1:T(8,128)(2,1)}), bf16[128,8,256]{0,2,1:T(8,128)(2,1)S(1)}, u32[]{:S(2)}, u32[]{:S(2)}) async-start(bf16[128,8,256]{0,2,1:T(8,128)(2,1)} %bitcast.6), calls=%async_computation.1 | async-start | bytes 1048576 | tf_op jit(solution)/shard_map/all_to_all | solution.py:151
  36.7 18.8 %all-to-all-start.4 = ((bf16[128,8,256]{0,2,1:T(8,128)(2,1)}), bf16[128,8,256]{0,2,1:T(8,128)(2,1)S(1)}, u32[]{:S(2)}, u32[]{:S(2)}) async-start(bf16[128,8,256]{0,2,1:T(8,128)(2,1)} %bitcast.20), calls=%async_computation.4 | async-start | bytes 1048576 | tf_op jit(solution)/shard_map/all_to_all | solution.py:150
  55.4 19.5 %all-to-all-start.3 = ((bf16[128,8,256]{0,2,1:T(8,128)(2,1)}), bf16[128,8,256]{0,2,1:T(8,128)(2,1)}, u32[]{:S(2)}, u32[]{:S(2)}) async-start(bf16[128,8,256]{0,2,1:T(8,128)(2,1)} %bitcast.15), calls=%async_computation.3 | async-start | bytes 1048576 | tf_op jit(solution)/shard_map/all_to_all | solution.py:152
  63.1 11.9 %copy-start.1 = (f32[1024,2,128]{0,2,1:T(8,128)}, f32[1024,2,128]{0,2,1:T(8,128)S(1)}, u32[]{:S(2)}) copy-start(f32[1024,2,128]{0,2,1:T(8,128)S(1)} %reshape.528) | copy-start | bytes 3145732
  75.0 27.3 %all-to-all-start.5 = ((bf16[128,8,256]{0,2,1:T(8,128)(2,1)}), bf16[128,8,256]{0,2,1:T(8,128)(2,1)}, u32[]{:S(2)}, u32[]{:S(2)}) async-start(bf16[128,8,256]{0,2,1:T(8,128)(2,1)} %bitcast.622), calls=%async_computation.5 | async-start | bytes 1048576 | tf_op jit(solution)/shard_map/all_to_all | solution.py:153
  84.0 1.5 copy-start.3
  107.4 5.0 copy-start
  788.1 2.7 copy-start.2
  792.7 10.1 %all-to-all-start.9 = ((bf16[8,128,2]{1,2,0:T(2,128)(2,1)}), bf16[8,128,2]{1,2,0:T(2,128)(2,1)S(1)}, u32[]{:S(2)}, u32[]{:S(2)}) async-start(bf16[8,128,2]{1,2,0:T(2,128)(2,1)} %fusion.167), calls=%async_computation.9 | async-start | bytes 8192 | tf_op jit(solution)/shard_map/all_to_all | solution.py:170
  802.8 9.3 %all-to-all-start.10 = ((bf16[8,128,2]{1,2,0:T(2,128)(2,1)}), bf16[8,128,2]{1,2,0:T(2,128)(2,1)S(1)}, u32[]{:S(2)}, u32[]{:S(2)}) async-start(bf16[8,128,2]{1,2,0:T(2,128)(2,1)} %bitcast.414), calls=%async_computation.10 | async-start | bytes 8192 | tf_op jit(solution)/shard_map/all_to_all | solution.py:173
  812.1 19.2 %all-to-all-start.7 = ((bf16[8,128,256]{1,2,0:T(8,128)(2,1)}), bf16[8,128,256]{1,2,0:T(8,128)(2,1)S(1)}, u32[]{:S(2)}, u32[]{:S(2)}) async-start(bf16[8,128,256]{1,2,0:T(8,128)(2,1)} %copy.378), calls=%async_computation.7 | async-start | bytes 1048576 | tf_op jit(solution)/shard_map/all_to_all | solution.py:168
  820.5 16.8 %copy-start.4 = (bf16[8,2,128,128]{3,2,0,1:T(8,128)(2,1)S(1)}, bf16[8,2,128,128]{3,2,0,1:T(8,128)(2,1)}, u32[]{:S(2)}) copy-start(bf16[8,2,128,128]{3,2,0,1:T(8,128)(2,1)} %get-tuple-element.1507) | copy-start | bytes 1572868
  831.2 18.8 %all-to-all-start.6 = ((bf16[8,128,256]{1,2,0:T(8,128)(2,1)}), bf16[8,128,256]{1,2,0:T(8,128)(2,1)S(1)}, u32[]{:S(2)}, u32[]{:S(2)}) async-start(bf16[8,128,256]{1,2,0:T(8,128)(2,1)} %copy.374), calls=%async_computation.6 | async-start | bytes 1048576 | tf_op jit(solution)/shard_map/all_to_all | solution.py:167
  850.0 18.8 %all-to-all-start.8 = ((bf16[8,128,256]{1,2,0:T(8,128)(2,1)}), bf16[8,128,256]{1,2,0:T(8,128)(2,1)S(1)}, u32[]{:S(2)}, u32[]{:S(2)}) async-start(bf16[8,128,256]{1,2,0:T(8,128)(2,1)} %copy.381), calls=%async_computation.8 | async-start | bytes 1048576 | tf_op jit(solution)/shard_map/all_to_all | solution.py:169
where the time goes:
time: 880 us; the launch traced here: 871 us
  other arithmetic  406 us (46%)
  matrix products  225 us (26%)
  local copies, waits for them, and re-layouts  77.7 us (9%)
  starting transfers between devices  67 us (8%)
  waiting for transfers between devices  65.8 us (7%)
  blocking collectives  26 us (3%)
    another operation x80, other arithmetic, group_step(): lax.linalg.triangular_solve(unit_lower, right_side, left_side=True, lower...  332 us
    dot_general x24, matrix products, group_step(): jnp.einsum('hid,hjd->hij', query_part, key_part, precision=precise)  38.8 us
    dynamic_update_slice x48, other arithmetic, block_forward(): lax.scan(group_step, (start_state, identity, grad_zero), inputs)  38.2 us
    dot_general x24, matrix products, group_step(): key_gram = jnp.einsum('hid,hjd->hij', key_part, key_part, precision=precise)  28.3 us
    dot_general x24, matrix products, group_step(): jnp.einsum('hcd,hde->hce', write_keys, state_now, precision=precise)  28.1 us
    dot_general x24, matrix products, group_step(): jnp.einsum('hcd,hce->hde', tail_keys, new_values, precision=precise)  25.2 us
    dot_general x16, matrix products, group_step(): jnp.einsum('hij,hje->hie', scores, new_values, precision=precise)  23.9 us
    dot_general x16, matrix products, group_step(): jnp.einsum('hcd,hde->hce', grown_queries, state_now, precision=precise)  21.9 us
  transfers between devices with their start and end apart: 10, of which 7 were waited for; matrix products, arithmetic and copies ran while one was open for 4% of the time, Pallas kernels for 0%

commit v1 on v0

v1 whole, which is shorter than its diff:
```python
import functools

import jax
import jax.numpy as jnp
from jax import lax
from jax.experimental import pallas as pl
from jax.experimental.pallas import tpu as pltpu
from jax.sharding import PartitionSpec as P

D = 128
C = 128
BF = jnp.bfloat16
F32 = jnp.float32
DIMS = {"nn": ((1,), (0,)), "nt": ((1,), (1,)), "tn": ((0,), (0,))}


def split(x):
    hi = x.astype(BF)
    return hi, (x - hi.astype(F32)).astype(BF)


def exact(x):
    return x.astype(BF), None


def dot(a, b, mode):
    return lax.dot_general(a, b, (DIMS[mode], ((), ())), preferred_element_type=F32)


def mm(a, b, mode):
    ka = 0 if mode == "tn" else 1
    kb = 1 if mode == "nt" else 0
    (ah, al), (bh, bl) = a, b
    if al is None and bl is None:
        return dot(ah, bh, mode)
    if al is None:
        return dot(jnp.concatenate([ah, ah], ka), jnp.concatenate([bh, bl], kb), mode)
    left = jnp.concatenate([ah, al], ka)
    if bl is None:
        return dot(left, jnp.concatenate([bh, bh], kb), mode)
    top = jnp.concatenate([bh, bl], 1 - kb)
    low = jnp.concatenate([bh, jnp.zeros_like(bl)], 1 - kb)
    both = dot(left, jnp.concatenate([top, low], kb), mode)
    n = both.shape[1] // 2
    return both[:, :n] + both[:, n:]


def iotas():
    return lax.broadcasted_iota(jnp.int32, (C, C), 0), lax.broadcasted_iota(jnp.int32, (C, C), 1)


def ones_where(mask):
    return jnp.where(mask, 1.0, 0.0).astype(BF)


def unit(x):
    r = lax.rsqrt(jnp.sum(x * x, axis=1, keepdims=True) + 1e-06)
    return x * r, r


def decays(gate, row, col):
    wide = jnp.broadcast_to(gate, (C, C))
    rhs = jnp.concatenate([wide, jnp.where(row > col, wide, 0.0)], 1).astype(BF)
    both = dot(ones_where(row >= col), rhs, "nn")
    after = dot(ones_where(row < col), wide.astype(BF), "nn")
    pair = jnp.where(row >= col, jnp.exp(both[:, C:]), 0.0)
    return jnp.exp(both[:, :C]), jnp.exp(after), pair


def inverses(lowers, row, col):
    eye = jnp.where(row == col, 1.0, 0.0)
    done = [eye - jnp.where((row // 2 == col // 2), low, 0.0) for low in lowers]
    size = 2
    while size < C:
        pick = (row // (2 * size) == col // (2 * size)) & (row // size != col // size)
        halves = [split(t) for t in done]
        mids = [mm(t, split(jnp.where(pick, low, 0.0)), "nn") for t, low in zip(halves, lowers)]
        done = [t - mm(split(m), h, "nn") for t, m, h in zip(done, mids, halves)]
        size *= 2
    return done


def first_kernel(
    hpd, ng, step,
    q_ref, k_ref, v_ref, c_ref, b_ref, g_ref, s0_ref,
    turned_ref, start_ref, inv_ref, wk_ref, wv_ref, pr_ref, pc_ref, dec_ref, gram_ref,
    st_ref, base_ref, suf_ref,
    m_ref, mt_ref, add_ref, radd_ref,
):
    row, col = iotas()
    eye = row == col

    def body(i, carry):
        units = [(i * step + s, h) for s in range(step) for h in range(hpd)]
        data = []
        lowers = []
        for g, h in units:
            rows = pl.ds(pl.multiple_of(g * C, C), C)
            cols = slice(h * D, (h + 1) * D)
            beta = jax.nn.sigmoid(jnp.broadcast_to(b_ref[rows, h : h + 1], (C, C)))
            growth, tail, pair = decays(g_ref[rows, h : h + 1], row, col)
            qn, _ = unit(q_ref[rows, cols].astype(F32))
            kn, _ = unit(k_ref[rows, cols].astype(F32))
            qs, ks = split(qn), split(kn)
            left = (jnp.concatenate([qs[0], ks[0]], 0), jnp.concatenate([qs[1], ks[1]], 0))
            grams = mm(left, ks, "nt")
            scores = grams[:C] * pair
            gram = jnp.where(row > col, grams[C:] * pair, 0.0)
            u = g * hpd + h
            dec_ref[u] = pair
            gram_ref[u] = gram
            pr_ref[u] = scores
            lowers.append(beta * gram)
            cot = exact(c_ref[rows, cols])
            pc = mm(split(scores), cot, "tn")
            pc_ref[u] = pc
            qpart = mm(split(qn * growth), cot, "tn")
            data.append((u, kn, beta, growth, tail, v_ref[rows, cols].astype(F32), pc, qpart))
        for inv, (u, kn, beta, growth, tail, val, pc, qpart) in zip(inverses(lowers, row, col), data):
            inv_ref[u] = inv
            halves = split(inv)
            wk = mm(halves, split(beta * growth * kn), "nn")
            wv = mm(halves, split(beta * val), "nn")
            wk_ref[u] = wk
            wv_ref[u] = wv
            ws, ts = split(wk), split(kn * tail)
            last = jnp.where(eye, jnp.broadcast_to(growth[C - 1 :, :], (C, C)), 0.0)
            m_ref[u] = last - mm(ts, ws, "tn")
            mt_ref[u] = last - mm(ws, ts, "tn")
            add_ref[u] = mm(ts, split(wv), "tn")
            radd_ref[u] = qpart - mm(ws, split(pc), "tn")
        return carry

    lax.fori_loop(0, ng // step, body, 0)

    def chain(i, carry):
        out = []
        for h in range(hpd):
            state, grad, suffix = carry[h]
            u, w = i * hpd + h, (ng - 1 - i) * hpd + h
            st_ref[u] = state
            base_ref[w] = grad
            suf_ref[w] = suffix
            turned = split(mt_ref[w])
            out.append((
                mm(split(m_ref[u]), split(state), "nn") + add_ref[u],
                mm(turned, split(grad), "nn") + radd_ref[w],
                mm(turned, split(suffix), "nn"),
            ))
        return tuple(out)

    init = tuple(
        (s0_ref[h], jnp.zeros((D, D), F32), jnp.where(eye, 1.0, 0.0)) for h in range(hpd)
    )
    final = lax.fori_loop(0, ng, chain, init)
    for h in range(hpd):
        turned_ref[h] = final[h][2]
        start_ref[h] = final[h][1]


def second_kernel(
    hpd, ng, step, n_outer,
    pos_ref, turned_ref, start_ref, q_ref, k_ref, v_ref, c_ref, b_ref, g_ref,
    inv_ref, wk_ref, wv_ref, pr_ref, pc_ref, dec_ref, gram_ref, st_ref, base_ref, suf_ref,
    dq_ref, dk_ref, dv_ref, db_ref, dg_ref,
):
    row, col = iotas()
    position = pos_ref[0]

    def fold(i, carry):
        b = n_outer - 1 - i
        return tuple(
            jnp.where(
                b > position,
                mm(split(turned_ref[b, h]), split(carry[h]), "nn") + start_ref[b, h],
                carry[h],
            )
            for h in range(hpd)
        )

    incoming = lax.fori_loop(
        0, n_outer - 1, fold, tuple(jnp.zeros((D, D), F32) for _ in range(hpd))
    )
    arriving = [split(x) for x in incoming]
    upper = ones_where(row <= col)
    upper2 = jnp.concatenate([upper, upper], 1)
    lower = ones_where(row > col)
    lower2 = jnp.concatenate([lower, lower], 1)

    def body(i, carry):
        for s in range(step):
            for h in range(hpd):
                g = i * step + s
                u = g * hpd + h
                rows = pl.ds(pl.multiple_of(g * C, C), C)
                cols = slice(h * D, (h + 1) * D)
                beta = jax.nn.sigmoid(jnp.broadcast_to(b_ref[rows, h : h + 1], (C, C)))
                wide = jnp.broadcast_to(g_ref[rows, h : h + 1], (C, C)).astype(BF)
                growth = jnp.exp(dot(ones_where(row >= col), wide, "nn"))
                tail = jnp.exp(dot(ones_where(row < col), wide, "nn"))
                qn, qr = unit(q_ref[rows, cols].astype(F32))
                kn, kr = unit(k_ref[rows, cols].astype(F32))
                val = v_ref[rows, cols].astype(F32)
                cot = exact(c_ref[rows, cols])
                state = st_ref[u]
                ss = split(state)
                after = base_ref[u] + mm(split(suf_ref[u]), arriving[h], "nn")
                fs = split(after)
                tk = kn * tail
                dnew = pc_ref[u] + mm(split(tk), fs, "nn")
                new = wv_ref[u] - mm(split(wk_ref[u]), ss, "nn")
                ns = split(new)
                err = mm(split(inv_ref[u]), split(dnew), "tn")
                es = split(err)
                dkw = -mm(es, ss, "nt")
                dlow = jnp.where(row > col, -mm(es, ns, "nt"), 0.0)
                dsc = mm(cot, ns, "nt")
                dqg = mm(cot, ss, "nt")
                dtk = mm(ns, fs, "nt")
                pair = dec_ref[u]
                gram = gram_ref[u]
                b1 = split(dsc * pair)
                b2 = split(dlow * beta * pair)
                qs, ks = split(qn), split(kn)
                b12 = (jnp.concatenate([b1[0], b2[0]], 0), jnp.concatenate([b1[1], b2[1]], 0))
                fwd = mm(b12, ks, "nn")
                dqn = fwd[:C] + growth * dqg
                dkn = (
                    fwd[C:] + mm(b1, qs, "tn") + mm(b2, ks, "tn")
                    + beta * growth * dkw + tail * dtk
                )
                dq_ref[rows, cols] = (
                    qr * (dqn - qn * jnp.sum(dqn * qn, axis=1, keepdims=True))
                ).astype(BF)
                dk_ref[rows, cols] = (
                    kr * (dkn - kn * jnp.sum(dkn * kn, axis=1, keepdims=True))
                ).astype(BF)
                dv_ref[rows, cols] = (beta * err).astype(BF)
                kgrow = kn * growth * dkw
                dlg = dlow * gram
                dbeta = jnp.sum(dlg + kgrow + err * val, axis=1, keepdims=True)
                b0 = beta[:, :1]
                db_ref[rows, h : h + 1] = dbeta * b0 * (1.0 - b0)
                z = dsc * pr_ref[u] + beta * dlg
                x = dqg * qn * growth + beta * kgrow
                y = dtk * tk
                zx = split(jnp.concatenate([z, x], 1))
                up = dot(upper2, jnp.concatenate(zx, 0), "nn")
                down = dot(lower2, jnp.concatenate(split(y), 0), "nn")
                total = jnp.sum(
                    jnp.sum(state * after * growth[C - 1 :, :], axis=1, keepdims=True),
                    axis=0, keepdims=True,
                )
                dg_ref[rows, h : h + 1] = (
                    jnp.sum(
                        jnp.where(row > col, up[:, :C], 0.0) + up[:, C:] + down,
                        axis=1, keepdims=True,
                    )
                    + total
                )
        return carry

    lax.fori_loop(0, ng // step, body, 0)


VM = pl.BlockSpec(memory_space=pltpu.VMEM)


def run_first(q, k, v, cot, logit, gate, s0, interpret=False):
    hpd, ng = q.shape[1] // D, q.shape[0] // C
    step = max(1, 4 // hpd)
    big = jax.ShapeDtypeStruct((hpd * ng, D, D), F32)
    small = jax.ShapeDtypeStruct((hpd, D, D), F32)
    return pl.pallas_call(
        functools.partial(first_kernel, hpd, ng, step),
        out_shape=(small, small) + (big,) * 10,
        in_specs=[VM] * 7,
        out_specs=(VM,) * 12,
        scratch_shapes=[pltpu.VMEM((hpd * ng, D, D), F32)] * 4,
        compiler_params=pltpu.CompilerParams(vmem_limit_bytes=56 << 20),
        interpret=interpret,
    )(q, k, v, cot, logit, gate, s0)


def run_second(pos, turned, start, q, k, v, cot, logit, gate, rest, interpret=False):
    hpd, ng = q.shape[1] // D, q.shape[0] // C
    step = max(1, 2 // hpd)
    big = jax.ShapeDtypeStruct(q.shape, BF)
    thin = jax.ShapeDtypeStruct((q.shape[0], hpd), F32)
    return pl.pallas_call(
        functools.partial(second_kernel, hpd, ng, step, turned.shape[0]),
        out_shape=(big, big, big, thin, thin),
        in_specs=[pl.BlockSpec(memory_space=pltpu.SMEM)] + [VM] * 18,
        out_specs=(VM,) * 5,
        compiler_params=pltpu.CompilerParams(vmem_limit_bytes=56 << 20),
        interpret=interpret,
    )(pos, turned, start, q, k, v, cot, logit, gate, *rest)


def shards(queries, key_rows, value_rows, beta_logit, log_gate, out_grad, block_states):
    def inward(x):
        return lax.all_to_all(x, "inner", split_axis=1, concat_axis=0, tiled=True)

    def outward(x):
        return lax.all_to_all(x, "inner", split_axis=0, concat_axis=1, tiled=True)

    q, k, v, cot = (inward(x) for x in (queries, key_rows, value_rows, out_grad))
    logit = inward(beta_logit).astype(F32)
    gate = inward(log_gate).astype(F32)
    first = run_first(q, k, v, cot, logit, gate, block_states[0])
    turned = lax.all_gather(first[0], "outer", axis=0)
    start = lax.all_gather(first[1], "outer", axis=0)
    pos = lax.axis_index("outer").astype(jnp.int32).reshape(1)
    out = run_second(pos, turned, start, q, k, v, cot, logit, gate, first[2:])
    return (
        outward(out[0]), outward(out[1]), outward(out[2]),
        outward(out[3].astype(BF)), outward(out[4].astype(BF)),
    )


def solution(mesh):
    wide = P(("outer", "inner"), None)
    return jax.shard_map(
        shards,
        mesh=mesh,
        in_specs=(wide,) * 6 + (P("outer", "inner", None, None),),
        out_specs=(wide,) * 5,
        check_vma=False,
    )
```

time: 880 us -> 244 us (0.28)
  other arithmetic: 406 us -> 1.16 us
  matrix products: 225 us -> 0 us
  local copies, waits for them, and re-layouts: 77.7 us -> 14.2 us
  Pallas kernels: 0 us -> 46.6 us
  blocking collectives: 26 us -> 71 us
  starting transfers between devices: 67 us -> 47.1 us
    another operation x122 -> x0, other arithmetic: 345 us -> none  [the longest x80 332 us: group_step(): lax.linalg.triangular_solve(unit_lower, right_side, left_side=True, lower...]
    dot_general x180 -> x0, matrix products: 210 us -> none  [the longest x24 38.8 us: group_step(): jnp.einsum('hid,hjd->hij', query_part, key_part, precision=precise)]
    pallas_call x0 -> x2, Pallas kernels: none -> 46.6 us  [the longest x1 23.5 us: run_first(): pl.pallas_call(functools.partial(first_kernel, hpd, ng, step), out_shape=...]
    all_to_all x1 -> x4, blocking collectives: 7.44 us -> 51.8 us  [the longest x3 44.5 us: outward(): return lax.all_to_all(x, 'inner', split_axis=0, concat_axis=1, tiled=True)]
    dynamic_update_slice x48 -> x0, other arithmetic: 38.2 us -> none  [block_forward(): lax.scan(group_step, (start_state, identity, grad_zero), inputs)]
    mul x34 -> x0, local copies, waits for them, and re-layouts: 19.9 us -> none  [the longest x8 5.42 us: group_step(): grown_queries = query_part * growth[:, :, None]]
    all_to_all x10 -> x7, starting transfers between devices: 67 us -> 47.1 us  [the longest x5 32.3 us: inward(): return lax.all_to_all(x, 'inner', split_axis=1, concat_axis=0, tiled=True)]
    transpose x10 -> x0, local copies, waits for them, and re-layouts: 16.9 us -> none  [the longest x6 13.1 us: to_groups(): return jnp.moveaxis(shaped, 1, 0)]
  transfers between devices with their start and end apart: 10 -> 7, of which waited for: 7 -> 6; matrix products, arithmetic and copies ran while one was open for 4% -> 3% of each run, Pallas kernels for 0% -> 0%
where the time goes in v1:
time: 244 us; the launch traced here: 240 us
  blocking collectives  71 us (29%)
  waiting for transfers between devices  58.8 us (24%)
  starting transfers between devices  47.1 us (19%)
  Pallas kernels  46.6 us (19%)
  local copies, waits for them, and re-layouts  14.2 us (6%)
    all_to_all x5, waiting for transfers between devices, inward(): return lax.all_to_all(x, 'inner', split_axis=1, concat_axis=0, tiled=True)  46.1 us
    all_to_all x3, blocking collectives, outward(): return lax.all_to_all(x, 'inner', split_axis=0, concat_axis=1, tiled=True)  44.5 us
    all_to_all x5, starting transfers between devices, inward(): return lax.all_to_all(x, 'inner', split_axis=1, concat_axis=0, tiled=True)  32.3 us
    pallas_call x1, Pallas kernels, run_first(): pl.pallas_call(functools.partial(first_kernel, hpd, ng, step), out_shape=...  23.5 us
    pallas_call x1, Pallas kernels, run_second(): pl.pallas_call(functools.partial(second_kernel, hpd, ng, step, turned.sha...  23.1 us
    all_to_all x2, starting transfers between devices, outward(): return lax.all_to_all(x, 'inner', split_axis=0, concat_axis=1, tiled=True)  14.8 us
    all_to_all x2, waiting for transfers between devices, outward(): return lax.all_to_all(x, 'inner', split_axis=0, concat_axis=1, tiled=True)  12.7 us
    all_gather x1, blocking collectives, shards(): turned = lax.all_gather(first[0], 'outer', axis=0)  11 us
  transfers between devices with their start and end apart: 7, of which 6 were waited for; matrix products, arithmetic and copies ran while one was open for 3% of the time, Pallas kernels for 0%

profile of v1, /device:TPU:25, one launch (start us, length us, event | category | flops | bytes accessed | tf_op | source)
XLA Modules:
  0.0 239.6 jit_solution(17038066762668540550)
XLA Ops:
  0.6 7.3 %all_to_all.197 = bf16[128,8,2]{0,2,1:T(2,128)(2,1)S(1)} all-to-all(bf16[128,8,2]{0,2,1:T(2,128)(2,1)} %bitcast.91), channel_id=1, replica_groups=mesh['outer'=4,'inner'=8] {'inner'}, dimensions={1} | all-to-all | bytes 8192 | tf_op jit(solution)/shard_map/all_to_all | solution.py:302
  7.9 6.8 %all-to-all-start.5 = ((bf16[128,8,2]{0,2,1:T(2,128)(2,1)}), bf16[128,8,2]{0,2,1:T(2,128)(2,1)S(1)}, u32[]{:S(2)}, u32[]{:S(2)}) async-start(bf16[128,8,2]{0,2,1:T(2,128)(2,1)} %bitcast.12), calls=%async_computation.5 | async-start | bytes 8192 | tf_op jit(solution)/shard_map/all_to_all | solution.py:302
  14.8 1.9 copy.48
  16.7 7.2 %all-to-all-start = ((bf16[128,8,256]{2,0,1:T(8,128)(2,1)}), bf16[128,8,256]{2,0,1:T(8,128)(2,1)S(1)}, u32[]{:S(2)}, u32[]{:S(2)}) async-start(bf16[128,8,256]{2,0,1:T(8,128)(2,1)} %bitcast.59), calls=%async_computation | async-start | bytes 1048576 | tf_op jit(solution)/shard_map/all_to_all | solution.py:302
  23.8 0.8 copy.47
  24.7 11.9 %all-to-all-done = bf16[128,8,256]{2,0,1:T(8,128)(2,1)S(1)} async-done(((bf16[128,8,256]{2,0,1:T(8,128)(2,1)}), bf16[128,8,256]{2,0,1:T(8,128)(2,1)S(1)}, u32[]{:S(2)}, u32[]{:S(2)}) %all-to-all-start) | async-done | bytes 524320 | tf_op jit(solution)/shard_map/all_to_all | solution.py:302
  37.3 6.1 %all-to-all-start.1 = ((bf16[128,8,256]{2,0,1:T(8,128)(2,1)}), bf16[128,8,256]{2,0,1:T(8,128)(2,1)S(1)}, u32[]{:S(2)}, u32[]{:S(2)}) async-start(bf16[128,8,256]{2,0,1:T(8,128)(2,1)} %bitcast.58), calls=%async_computation.1 | async-start | bytes 1048576 | tf_op jit(solution)/shard_map/all_to_all | solution.py:302
  43.4 0.8 copy.46
  44.2 11.9 %all-to-all-done.1 = bf16[128,8,256]{2,0,1:T(8,128)(2,1)S(1)} async-done(((bf16[128,8,256]{2,0,1:T(8,128)(2,1)}), bf16[128,8,256]{2,0,1:T(8,128)(2,1)S(1)}, u32[]{:S(2)}, u32[]{:S(2)}) %all-to-all-start.1) | async-done | bytes 524320 | tf_op jit(solution)/shard_map/all_to_all | solution.py:302
  56.9 6.1 %all-to-all-start.2 = ((bf16[128,8,256]{2,0,1:T(8,128)(2,1)}), bf16[128,8,256]{2,0,1:T(8,128)(2,1)S(1)}, u32[]{:S(2)}, u32[]{:S(2)}) async-start(bf16[128,8,256]{2,0,1:T(8,128)(2,1)} %bitcast.57), calls=%async_computation.2 | async-start | bytes 1048576 | tf_op jit(solution)/shard_map/all_to_all | solution.py:302
  63.0 0.8 copy.45
  63.8 11.8 %all-to-all-done.2 = bf16[128,8,256]{2,0,1:T(8,128)(2,1)S(1)} async-done(((bf16[128,8,256]{2,0,1:T(8,128)(2,1)}), bf16[128,8,256]{2,0,1:T(8,128)(2,1)S(1)}, u32[]{:S(2)}, u32[]{:S(2)}) %all-to-all-start.2) | async-done | bytes 524320 | tf_op jit(solution)/shard_map/all_to_all | solution.py:302
  75.7 0.8 copy-done.2
  76.5 6.1 %all-to-all-start.3 = ((bf16[128,8,256]{2,0,1:T(8,128)(2,1)}), bf16[128,8,256]{2,0,1:T(8,128)(2,1)S(1)}, u32[]{:S(2)}, u32[]{:S(2)}) async-start(bf16[128,8,256]{2,0,1:T(8,128)(2,1)} %bitcast.56), calls=%async_computation.3 | async-start | bytes 1048576 | tf_op jit(solution)/shard_map/all_to_all | solution.py:302
  82.6 1.0 copy.28
  83.6 1.1 copy.27
  84.7 10.6 %all-to-all-done.3 = bf16[128,8,256]{2,0,1:T(8,128)(2,1)S(1)} async-done(((bf16[128,8,256]{2,0,1:T(8,128)(2,1)}), bf16[128,8,256]{2,0,1:T(8,128)(2,1)S(1)}, u32[]{:S(2)}, u32[]{:S(2)}) %all-to-all-start.3) | async-done | bytes 524320 | tf_op jit(solution)/shard_map/all_to_all | solution.py:302
  96.0 23.5 %shard_map.110 = (f32[2,128,128]{2,1,0:T(8,128)}, f32[2,128,128]{2,1,0:T(8,128)}, f32[16,128,128]{2,1,0:T(8,128)}, f32[16,128,128]{2,1,0:T(8,128)}, f32[16,128,1...) custom-call(bf16[1024,256]{1,0:T(8,128)(2,1)} %bitcast.60, ...), custom_call_target="tpu_custom_call" | custom-call | tf_op jit(solution)/shard_map/pallas_call | solution.py:274
  119.6 11.0 %all-gather = f32[8,128,128]{2,1,0:T(8,128)} all-gather(f32[2,128,128]{2,1,0:T(8,128)} %get-tuple-element.22), channel_id=2, replica_groups=mesh['outer'=4,'inner'=8] {'outer'}, dimensions={0}, use_global_device_ids=true | all-gather | bytes 655360 | tf_op jit(solution)/shard_map/all_gather | solution.py:311
  130.6 8.2 %all-gather.1 = f32[8,128,128]{2,1,0:T(8,128)} all-gather(f32[2,128,128]{2,1,0:T(8,128)S(1)} %copy-done.10), channel_id=3, replica_groups=mesh['outer'=4,'inner'=8] {'outer'}, dimensions={0}, use_global_device_ids=true | all-gather | bytes 655360 | tf_op jit(solution)/shard_map/all_gather | solution.py:312
  138.7 23.1 %shard_map.111 = (bf16[1024,256]{1,0:T(8,128)(2,1)}, bf16[1024,256]{1,0:T(8,128)(2,1)}, bf16[1024,256]{1,0:T(8,128)(2,1)}, f32[1024,2]{1,0:T(8,128)}, f32[1024,2]{1,0:T(8,128)}) custom-call(s32[1]{0:T(128)} %bitcast.pos_ref, f32[4,2,128,128]{3,2,1,0:T(8,128)} %bitcast.72, f32[4,2,128,128]{3,2,1,0:T(8,128)} %bitcast.73, bf16[1024,256]{1,0:T(8,128)(2,1)} %bitcast.61, ...), custom_call_target="tpu_custom_call" | custom-call | tf_op jit(solution)/shard_map/pallas_call | solution.py:290
  161.9 1.1 convert_element_type.26
  163.7 8.7 %all-to-all-start.9 = ((bf16[8,128,2]{1,2,0:T(2,128)(2,1)}), bf16[8,128,2]{1,2,0:T(2,128)(2,1)S(1)}, u32[]{:S(2)}, u32[]{:S(2)}) async-start(bf16[8,128,2]{1,2,0:T(2,128)(2,1)} %copy.32), calls=%async_computation.9 | async-start | bytes 8192 | tf_op jit(solution)/shard_map/all_to_all | solution.py:305
  172.6 1.7 all-to-all-done.9
  174.3 7.9 %all_to_all.198 = bf16[8,128,2]{1,2,0:T(2,128)(2,1)S(1)} all-to-all(bf16[8,128,2]{1,2,0:T(2,128)(2,1)S(1)} %copy.33), channel_id=1, replica_groups=mesh['outer'=4,'inner'=8] {'inner'}, dimensions={0} | all-to-all | bytes 8192 | tf_op jit(solution)/shard_map/all_to_all | solution.py:305
  182.2 18.8 %all_to_all.199 = bf16[8,128,256]{2,1,0:T(8,128)(2,1)S(1)} all-to-all(bf16[8,128,256]{2,1,0:T(8,128)(2,1)S(1)} %bitcast.84), channel_id=1, replica_groups=mesh['outer'=4,'inner'=8] {'inner'}, dimensions={0} | all-to-all | bytes 1048576 | tf_op jit(solution)/shard_map/all_to_all | solution.py:305
  201.1 17.8 %all_to_all.200 = bf16[8,128,256]{2,1,0:T(8,128)(2,1)S(1)} all-to-all(bf16[8,128,256]{2,1,0:T(8,128)(2,1)S(1)} %bitcast.83), channel_id=1, replica_groups=mesh['outer'=4,'inner'=8] {'inner'}, dimensions={0} | all-to-all | bytes 1048576 | tf_op jit(solution)/shard_map/all_to_all | solution.py:305
  218.8 6.1 %all-to-all-start.8 = ((bf16[8,128,256]{2,1,0:T(8,128)(2,1)}), bf16[8,128,256]{2,1,0:T(8,128)(2,1)S(1)}, u32[]{:S(2)}, u32[]{:S(2)}) async-start(bf16[8,128,256]{2,1,0:T(8,128)(2,1)} %bitcast.22), calls=%async_computation.8 | async-start | bytes 1048576 | tf_op jit(solution)/shard_map/all_to_all | solution.py:305
  224.9 0.8 copy.39
  225.8 0.8 copy.38
  226.6 11.0 %all-to-all-done.8 = bf16[8,128,256]{2,1,0:T(8,128)(2,1)S(1)} async-done(((bf16[8,128,256]{2,1,0:T(8,128)(2,1)}), bf16[8,128,256]{2,1,0:T(8,128)(2,1)S(1)}, u32[]{:S(2)}, u32[]{:S(2)}) %all-to-all-start.8) | async-done | bytes 524320 | tf_op jit(solution)/shard_map/all_to_all | solution.py:305
  237.6 0.8 copy.40
  (29 shorter events, 4.5 us)
Async XLA Ops:
  7.9 8.7 %all-to-all-start.5 = ((bf16[128,8,2]{0,2,1:T(2,128)(2,1)}), bf16[128,8,2]{0,2,1:T(2,128)(2,1)S(1)}, u32[]{:S(2)}, u32[]{:S(2)}) async-start(bf16[128,8,2]{0,2,1:T(2,128)(2,1)} %bitcast.12), calls=%async_computation.5 | async-start | bytes 8192 | tf_op jit(solution)/shard_map/all_to_all | solution.py:302
  16.7 7.2 %copy-start.5 = (bf16[128,2048]{1,0:T(8,128)(2,1)S(1)}, bf16[128,2048]{1,0:T(8,128)(2,1)}, u32[]{:S(2)}) copy-start(bf16[128,2048]{1,0:T(8,128)(2,1)} %param.8) | copy-start | bytes 1572868
  16.7 19.9 %all-to-all-start = ((bf16[128,8,256]{2,0,1:T(8,128)(2,1)}), bf16[128,8,256]{2,0,1:T(8,128)(2,1)S(1)}, u32[]{:S(2)}, u32[]{:S(2)}) async-start(bf16[128,8,256]{2,0,1:T(8,128)(2,1)} %bitcast.59), calls=%async_computation | async-start | bytes 1048576 | tf_op jit(solution)/shard_map/all_to_all | solution.py:302
  36.5 0.8 copy-start
  36.5 6.9 %copy-start.6 = (bf16[128,2048]{1,0:T(8,128)(2,1)S(1)}, bf16[128,2048]{1,0:T(8,128)(2,1)}, u32[]{:S(2)}) copy-start(bf16[128,2048]{1,0:T(8,128)(2,1)} %param.9) | copy-start | bytes 1572868
  37.3 18.8 %all-to-all-start.1 = ((bf16[128,8,256]{2,0,1:T(8,128)(2,1)}), bf16[128,8,256]{2,0,1:T(8,128)(2,1)S(1)}, u32[]{:S(2)}, u32[]{:S(2)}) async-start(bf16[128,8,256]{2,0,1:T(8,128)(2,1)} %bitcast.58), calls=%async_computation.1 | async-start | bytes 1048576 | tf_op jit(solution)/shard_map/all_to_all | solution.py:302
  56.1 0.8 copy-start.1
  56.1 6.9 %copy-start.7 = (bf16[128,2048]{1,0:T(8,128)(2,1)S(1)}, bf16[128,2048]{1,0:T(8,128)(2,1)}, u32[]{:S(2)}) copy-start(bf16[128,2048]{1,0:T(8,128)(2,1)} %param.12) | copy-start | bytes 1572868
  56.9 18.8 %all-to-all-start.2 = ((bf16[128,8,256]{2,0,1:T(8,128)(2,1)}), bf16[128,8,256]{2,0,1:T(8,128)(2,1)S(1)}, u32[]{:S(2)}, u32[]{:S(2)}) async-start(bf16[128,8,256]{2,0,1:T(8,128)(2,1)} %bitcast.57), calls=%async_computation.2 | async-start | bytes 1048576 | tf_op jit(solution)/shard_map/all_to_all | solution.py:302
  75.7 0.8 copy-start.2
  76.5 18.8 %all-to-all-start.3 = ((bf16[128,8,256]{2,0,1:T(8,128)(2,1)}), bf16[128,8,256]{2,0,1:T(8,128)(2,1)S(1)}, u32[]{:S(2)}, u32[]{:S(2)}) async-start(bf16[128,8,256]{2,0,1:T(8,128)(2,1)} %bitcast.56), calls=%async_computation.3 | async-start | bytes 1048576 | tf_op jit(solution)/shard_map/all_to_all | solution.py:302
  95.2 0.8 copy-start.3
  119.5 11.0 %copy-start.10 = (f32[2,128,128]{2,1,0:T(8,128)S(1)}, f32[2,128,128]{2,1,0:T(8,128)}, u32[]{:S(2)}) copy-start(f32[2,128,128]{2,1,0:T(8,128)} %get-tuple-element.23) | copy-start | bytes 393220
  161.9 10.6 %copy-start.4 = (f32[1024,2]{1,0:T(8,128)S(1)}, f32[1024,2]{1,0:T(8,128)}, u32[]{:S(2)}) copy-start(f32[1024,2]{1,0:T(8,128)} %get-tuple-element.38) | copy-start | bytes 24580
  163.7 10.6 %all-to-all-start.9 = ((bf16[8,128,2]{1,2,0:T(2,128)(2,1)}), bf16[8,128,2]{1,2,0:T(2,128)(2,1)S(1)}, u32[]{:S(2)}, u32[]{:S(2)}) async-start(bf16[8,128,2]{1,2,0:T(2,128)(2,1)} %copy.32), calls=%async_computation.9 | async-start | bytes 8192 | tf_op jit(solution)/shard_map/all_to_all | solution.py:305
  172.4 9.8 %copy-start.9 = (bf16[1024,256]{1,0:T(8,128)(2,1)S(1)}, bf16[1024,256]{1,0:T(8,128)(2,1)}, u32[]{:S(2)}) copy-start(bf16[1024,256]{1,0:T(8,128)(2,1)} %get-tuple-element.35) | copy-start | bytes 1572868
  182.2 18.8 %copy-start.8 = (bf16[1024,256]{1,0:T(8,128)(2,1)S(1)}, bf16[1024,256]{1,0:T(8,128)(2,1)}, u32[]{:S(2)}) copy-start(bf16[1024,256]{1,0:T(8,128)(2,1)} %get-tuple-element.34) | copy-start | bytes 1572868
  218.8 18.8 %all-to-all-start.8 = ((bf16[8,128,256]{2,1,0:T(8,128)(2,1)}), bf16[8,128,256]{2,1,0:T(8,128)(2,1)S(1)}, u32[]{:S(2)}, u32[]{:S(2)}) async-start(bf16[8,128,256]{2,1,0:T(8,128)(2,1)} %bitcast.22), calls=%async_computation.8 | async-start | bytes 1048576 | tf_op jit(solution)/shard_map/all_to_all | solution.py:305

commit v2 on v1

v2 whole, which is shorter than its diff:
```python
import functools

import jax
import jax.numpy as jnp
from jax import lax
from jax.experimental import pallas as pl
from jax.experimental.pallas import tpu as pltpu
from jax.sharding import PartitionSpec as P

D = 128
C = 128
BF = jnp.bfloat16
F32 = jnp.float32
MESH = pl.DeviceIdType.MESH
VM = pl.BlockSpec(memory_space=pltpu.VMEM)
DIMS = {"nn": ((1,), (0,)), "nt": ((1,), (1,)), "tn": ((0,), (0,))}


def split(x):
    hi = x.astype(BF)
    return hi, (x - hi.astype(F32)).astype(BF)


def exact(x):
    return x.astype(BF), None


def dot(a, b, mode):
    return lax.dot_general(a, b, (DIMS[mode], ((), ())), preferred_element_type=F32)


def mm(a, b, mode):
    ka = 0 if mode == "tn" else 1
    kb = 1 if mode == "nt" else 0
    (ah, al), (bh, bl) = a, b
    if al is None and bl is None:
        return dot(ah, bh, mode)
    if al is None:
        return dot(jnp.concatenate([ah, ah], ka), jnp.concatenate([bh, bl], kb), mode)
    left = jnp.concatenate([ah, al], ka)
    if bl is None:
        return dot(left, jnp.concatenate([bh, bh], kb), mode)
    top = jnp.concatenate([bh, bl], 1 - kb)
    low = jnp.concatenate([bh, jnp.zeros_like(bl)], 1 - kb)
    both = dot(left, jnp.concatenate([top, low], kb), mode)
    n = both.shape[1] // 2
    return both[:, :n] + both[:, n:]


def iotas():
    return lax.broadcasted_iota(jnp.int32, (C, C), 0), lax.broadcasted_iota(jnp.int32, (C, C), 1)


def ones_where(mask):
    return jnp.where(mask, 1.0, 0.0).astype(BF)


def unit(x):
    r = lax.rsqrt(jnp.sum(x * x, axis=1, keepdims=True) + 1e-06)
    return x * r, r


def decays(gate, row, col):
    wide = gate
    rhs = jnp.concatenate([wide, jnp.where(row > col, wide, 0.0)], 1).astype(BF)
    both = dot(ones_where(row >= col), rhs, "nn")
    after = dot(ones_where(row < col), wide.astype(BF), "nn")
    pair = jnp.where(row >= col, jnp.exp(both[:, C:]), 0.0)
    return jnp.exp(both[:, :C]), jnp.exp(after), pair


def inverses(lowers, row, col):
    eye = jnp.where(row == col, 1.0, 0.0)
    done = [eye - jnp.where((row // 2 == col // 2), low, 0.0) for low in lowers]
    size = 2
    while size < C:
        pick = (row // (2 * size) == col // (2 * size)) & (row // size != col // size)
        halves = [split(t) for t in done]
        mids = [mm(t, split(jnp.where(pick, low, 0.0)), "nn") for t, low in zip(halves, lowers)]
        done = [t - mm(split(m), h, "nn") for t, m, h in zip(done, mids, halves)]
        size *= 2
    return done


def head_columns(b_ref, g_ref, h):
    heads = b_ref.shape[1]
    pick = ones_where(lax.broadcasted_iota(jnp.int32, (heads, C), 0) == h)
    return jax.nn.sigmoid(dot(b_ref[...], pick, "nn")), dot(g_ref[...], pick, "nn")


def grams(qn, kn, pair, row, col):
    qs, ks = split(qn), split(kn)
    left = (jnp.concatenate([qs[0], ks[0]], 0), jnp.concatenate([qs[1], ks[1]], 0))
    both = mm(left, ks, "nt")
    return both[:C] * pair, jnp.where(row > col, both[C:] * pair, 0.0)


def first_kernel(
    count, b_ref, g_ref, q_ref, k_ref, v_ref, c_ref,
    m_ref, mt_ref, add_ref, radd_ref, inv_ref, wk_ref, wv_ref, pc_ref,
):
    row, col = iotas()
    eye = row == col
    data, lowers = [], []
    for s in range(count):
        cols = slice(s * D, (s + 1) * D)
        beta, gate = head_columns(b_ref, g_ref, pl.program_id(0) * count + s)
        growth, tail, pair = decays(gate, row, col)
        qn, _ = unit(q_ref[:, cols].astype(F32))
        kn, _ = unit(k_ref[:, cols].astype(F32))
        scores, gram = grams(qn, kn, pair, row, col)
        lowers.append(beta * gram)
        cot = exact(c_ref[:, cols])
        pc = mm(split(scores), cot, "tn")
        pc_ref[s] = pc
        qpart = mm(split(qn * growth), cot, "tn")
        data.append((kn, beta, growth, tail, v_ref[:, cols].astype(F32), pc, qpart))
    for s, inv in enumerate(inverses(lowers, row, col)):
        kn, beta, growth, tail, val, pc, qpart = data[s]
        inv_ref[s] = inv
        halves = split(inv)
        wk = mm(halves, split(beta * growth * kn), "nn")
        wv = mm(halves, split(beta * val), "nn")
        wk_ref[s] = wk
        wv_ref[s] = wv
        ws, ts = split(wk), split(kn * tail)
        last = jnp.where(eye, jnp.broadcast_to(growth[C - 1 :, :], (C, C)), 0.0)
        m_ref[s] = last - mm(ts, ws, "tn")
        mt_ref[s] = last - mm(ws, ts, "tn")
        add_ref[s] = mm(ts, split(wv), "tn")
        radd_ref[s] = qpart - mm(ws, split(pc), "tn")


def chain_kernel(
    heads, n, n_outer,
    s0_ref, m_ref, mt_ref, add_ref, radd_ref,
    st_ref, after_ref,
    sout, bin_ref, bout, oin, oout,
    s0send, fsend, frecv, bsend, brecv, osend, orecv, rsend,
):
    o, i = lax.axis_index("outer"), lax.axis_index("inner")
    hpd = s0_ref.shape[0]
    barrier = pltpu.get_barrier_semaphore()
    for d in range(1, n):
        pl.semaphore_signal(
            barrier, inc=1, device_id=(o, lax.rem(i + d, n)), device_id_type=MESH
        )
    for d in range(1, n_outer):
        pl.semaphore_signal(
            barrier, inc=1, device_id=(lax.rem(o + d, n_outer), i), device_id_type=MESH
        )
    pl.semaphore_wait(barrier, n + n_outer - 2)

    def remote(src, dst, send, recv, target):
        return pltpu.make_async_remote_copy(
            src_ref=src, dst_ref=dst, send_sem=send, recv_sem=recv,
            device_id=target, device_id_type=MESH,
        )

    def start_copy(j):
        h = i * hpd + j
        return remote(s0_ref.at[j], st_ref.at[h], s0send.at[j], frecv.at[h], (o, 0))

    def up_copy(h):
        return remote(sout.at[h], st_ref.at[h], fsend.at[h], frecv.at[h], (o, lax.rem(i + 1, n)))

    def down_copy(h):
        return remote(
            bout.at[h], bin_ref.at[h], bsend.at[h], brecv.at[h], (o, lax.rem(i + n - 1, n))
        )

    def outer_copy(h):
        return remote(
            oout.at[h], oin.at[h], osend.at[h], orecv.at[h],
            (lax.rem(o + n_outer - 1, n_outer), i),
        )

    def relay_copy(h, hop):
        return remote(
            oin.at[h], oin.at[h], rsend.at[h, hop - 1], orecv.at[h], (o, lax.rem(i + hop, n))
        )

    even = lax.rem(i, 2) == 0
    relays = o < n_outer - 1
    near = relays & even & (i + 1 < n)
    far = relays & even & (i + 2 < n)

    @pl.when(i == 0)
    def _():
        for j in range(hpd):
            pltpu.make_async_copy(s0_ref.at[j], st_ref.at[j], frecv.at[j]).start()

    @pl.when(i > 0)
    def _():
        for j in range(hpd):
            start_copy(j).start()

    lag_up = 2 * i
    lag_down = 2 * (n - 1 - i)
    lag_outer = 2 * (n - 1) + 2 * (n_outer - 1 - o)
    lag_in = lag_outer + 2 * (i // 2 + lax.rem(i, 2))

    def tick(t, carry):
        up = t - lag_up

        @pl.when((up >= 0) & (up < heads))
        def _():
            pltpu.make_async_copy(st_ref.at[up], st_ref.at[up], frecv.at[up]).wait()

            @pl.when(i < n - 1)
            def _():
                sout[up] = mm(split(m_ref[up]), split(st_ref[up]), "nn") + add_ref[up]
                up_copy(up).start()

        down = t - lag_down

        @pl.when((down >= 0) & (down < heads))
        def _():
            @pl.when(i == n - 1)
            def _():
                row, col = iotas()
                bin_ref[down, :, :D] = jnp.zeros((D, D), F32)
                bin_ref[down, :, D:] = jnp.where(row == col, 1.0, 0.0)
                bout[down, :, :D] = radd_ref[down]
                bout[down, :, D:] = mt_ref[down]

            @pl.when(i < n - 1)
            def _():
                down_copy(down).wait_recv()
                turned = split(mt_ref[down])
                bout[down, :, :D] = (
                    mm(turned, split(bin_ref[down, :, :D]), "nn") + radd_ref[down]
                )
                bout[down, :, D:] = mm(turned, split(bin_ref[down, :, D:]), "nn")

            @pl.when(i > 0)
            def _():
                down_copy(down).start()

        last = t - lag_in

        @pl.when((last >= 0) & (last < heads))
        def _():
            @pl.when(relays)
            def _():
                outer_copy(last).wait_recv()

            @pl.when(near)
            def _():
                relay_copy(last, 1).start()

            @pl.when(far)
            def _():
                relay_copy(last, 2).start()

            @pl.when((i == 0) & (o > 0) & relays)
            def _():
                oout[last] = (
                    mm(split(bout[last, :, D:]), split(oin[last]), "nn") + bout[last, :, :D]
                )

            @pl.when((i == 0) & (o > 0) & (o == n_outer - 1))
            def _():
                oout[last] = bout[last, :, :D]

            @pl.when((i == 0) & (o > 0))
            def _():
                outer_copy(last).start()

            @pl.when(relays)
            def _():
                after_ref[last] = bin_ref[last, :, :D] + mm(
                    split(bin_ref[last, :, D:]), split(oin[last]), "nn"
                )

            @pl.when(o == n_outer - 1)
            def _():
                after_ref[last] = bin_ref[last, :, :D]

        return carry

    ticks = heads + 2 * (n - 1) + 2 * (n_outer - 1) + 2 * ((n - 1) // 2 + (n - 1) % 2)
    lax.fori_loop(0, ticks, tick, 0)

    @pl.when(i > 0)
    def _():
        for j in range(hpd):
            start_copy(j).wait_send()

    def finish(h, carry):
        @pl.when(i < n - 1)
        def _():
            up_copy(h).wait_send()

        @pl.when(i > 0)
        def _():
            down_copy(h).wait_send()

        @pl.when((i == 0) & (o > 0))
        def _():
            outer_copy(h).wait_send()

        @pl.when(near)
        def _():
            relay_copy(h, 1).wait_send()

        @pl.when(far)
        def _():
            relay_copy(h, 2).wait_send()

        return carry

    lax.fori_loop(0, heads, finish, 0)


def final_kernel(
    count, b_ref, g_ref, q_ref, k_ref, v_ref, c_ref,
    inv_ref, wk_ref, wv_ref, pc_ref, st_ref, after_ref,
    dq_ref, dk_ref, dv_ref, db_ref, dg_ref, db_acc, dg_acc,
):
    row, col = iotas()
    step = pl.program_id(0)

    @pl.when(step == 0)
    def _():
        db_acc[...] = jnp.zeros_like(db_acc)
        dg_acc[...] = jnp.zeros_like(dg_acc)

    upper = ones_where(row <= col)
    upper2 = jnp.concatenate([upper, upper], 1)
    lower = ones_where(row > col)
    lower2 = jnp.concatenate([lower, lower], 1)
    lane = lax.broadcasted_iota(jnp.int32, db_acc.shape, 1)
    for s in range(count):
        cols = slice(s * D, (s + 1) * D)
        h = step * count + s
        beta, gate = head_columns(b_ref, g_ref, h)
        growth, tail, pair = decays(gate, row, col)
        qn, qr = unit(q_ref[:, cols].astype(F32))
        kn, kr = unit(k_ref[:, cols].astype(F32))
        scores, gram = grams(qn, kn, pair, row, col)
        val = v_ref[:, cols].astype(F32)
        cot = exact(c_ref[:, cols])
        state, after = st_ref[s], after_ref[s]
        ss, fs = split(state), split(after)
        tk = kn * tail
        new = wv_ref[s] - mm(split(wk_ref[s]), ss, "nn")
        ns = split(new)
        dsc = mm(cot, ns, "nt")
        dqg = mm(cot, ss, "nt")
        dnew = pc_ref[s] + mm(split(tk), fs, "nn")
        err = mm(split(inv_ref[s]), split(dnew), "tn")
        es = split(err)
        dkw = -mm(es, ss, "nt")
        dlow = jnp.where(row > col, -mm(es, ns, "nt"), 0.0)
        dtk = mm(ns, fs, "nt")
        b1 = split(dsc * pair)
        b2 = split(dlow * beta * pair)
        qs, ks = split(qn), split(kn)
        b12 = (jnp.concatenate([b1[0], b2[0]], 0), jnp.concatenate([b1[1], b2[1]], 0))
        fwd = mm(b12, ks, "nn")
        dqn = fwd[:C] + growth * dqg
        dkn = (
            fwd[C:] + mm(b1, qs, "tn") + mm(b2, ks, "tn") + beta * growth * dkw + tail * dtk
        )
        dq_ref[:, cols] = (qr * (dqn - qn * jnp.sum(dqn * qn, axis=1, keepdims=True))).astype(BF)
        dk_ref[:, cols] = (kr * (dkn - kn * jnp.sum(dkn * kn, axis=1, keepdims=True))).astype(BF)
        dv_ref[:, cols] = (beta * err).astype(BF)
        kgrow = kn * growth * dkw
        dlg = dlow * gram
        dbeta = jnp.sum((dlg + kgrow + err * val) * (beta * (1.0 - beta)), axis=1, keepdims=True)
        z = dsc * scores + beta * dlg
        x = dqg * qn * growth + beta * kgrow
        zx = split(jnp.concatenate([z, x], 1))
        up = dot(upper2, jnp.concatenate(zx, 0), "nn")
        below = dot(lower2, jnp.concatenate(split(dtk * tk), 0), "nn")
        total = jnp.sum(
            jnp.sum(state * after * growth[C - 1 :, :], axis=1, keepdims=True),
            axis=0, keepdims=True,
        )
        dgate = total + jnp.sum(
            jnp.where(row > col, up[:, :C], 0.0) + up[:, C:] + below, axis=1, keepdims=True
        )
        db_acc[...] = jnp.where(lane == h, dbeta, db_acc[...])
        dg_acc[...] = jnp.where(lane == h, dgate, dg_acc[...])

    @pl.when(step == pl.num_programs(0) - 1)
    def _():
        db_ref[...] = db_acc[...].astype(BF)
        dg_ref[...] = dg_acc[...].astype(BF)


def head_specs(count, heads):
    small = pl.BlockSpec((C, heads), lambda j: (0, 0))
    token = pl.BlockSpec((C, count * D), lambda j: (0, j))
    matrix = pl.BlockSpec((count, D, D), lambda j: (j, 0, 0))
    return small, token, matrix


PARAMS = pltpu.CompilerParams(vmem_limit_bytes=56 << 20)


def run_first(logit, gate, q, k, v, cot, count=4, interpret=False):
    heads = logit.shape[1]
    small, token, matrix = head_specs(count, heads)
    big = jax.ShapeDtypeStruct((heads, D, D), F32)
    return pl.pallas_call(
        functools.partial(first_kernel, count),
        grid=(heads // count,),
        out_shape=(big,) * 8,
        in_specs=[small] * 2 + [token] * 4,
        out_specs=(matrix,) * 8,
        compiler_params=PARAMS,
        interpret=interpret,
    )(logit, gate, q, k, v, cot)


def run_chain(s0, m, mt, add, radd, n, n_outer):
    heads = m.shape[0]
    big = jax.ShapeDtypeStruct((heads, D, D), F32)
    one = pltpu.VMEM((heads, D, D), F32)
    two = pltpu.VMEM((heads, D, 2 * D), F32)
    sems = pltpu.SemaphoreType.DMA((heads,))
    return pl.pallas_call(
        functools.partial(chain_kernel, heads, n, n_outer),
        out_shape=(big, big),
        in_specs=[VM] * 5,
        out_specs=(VM, VM),
        scratch_shapes=[
            one, two, two, one, one,
            pltpu.SemaphoreType.DMA((s0.shape[0],)), sems, sems, sems, sems, sems, sems,
            pltpu.SemaphoreType.DMA((heads, 2)),
        ],
        compiler_params=pltpu.CompilerParams(
            vmem_limit_bytes=56 << 20, collective_id=0, has_side_effects=True
        ),
    )(s0, m, mt, add, radd)


def run_final(logit, gate, q, k, v, cot, rest, count=2, interpret=False):
    heads = logit.shape[1]
    small, token, matrix = head_specs(count, heads)
    big = jax.ShapeDtypeStruct(q.shape, BF)
    thin = jax.ShapeDtypeStruct(logit.shape, BF)
    return pl.pallas_call(
        functools.partial(final_kernel, count),
        grid=(heads // count,),
        out_shape=(big, big, big, thin, thin),
        in_specs=[small] * 2 + [token] * 4 + [matrix] * 6,
        out_specs=(token, token, token, small, small),
        scratch_shapes=[pltpu.VMEM((C, heads), F32)] * 2,
        compiler_params=PARAMS,
        interpret=interpret,
    )(logit, gate, q, k, v, cot, *rest)


def shards(n, n_outer, queries, key_rows, value_rows, beta_logit, log_gate, out_grad, block_states):
    tokens = (beta_logit, log_gate, queries, key_rows, value_rows, out_grad)
    m, mt, add, radd, inv, wk, wv, pc = run_first(*tokens)
    state, after = run_chain(block_states[0], m, mt, add, radd, n, n_outer)
    return run_final(*tokens, (inv, wk, wv, pc, state, after))


def solution(mesh):
    wide = P(("outer", "inner"), None)
    return jax.shard_map(
        functools.partial(shards, mesh.shape["inner"], mesh.shape["outer"]),
        mesh=mesh,
        in_specs=(wide,) * 6 + (P("outer", "inner", None, None),),
        out_specs=(wide,) * 5,
        check_vma=False,
    )
```

time: 244 us -> 116 us (0.48); the launches traced: 240 us -> 115 us
  blocking collectives: 71 us -> 0 us
  Pallas kernels: 46.6 us -> 110 us
  waiting for transfers between devices: 58.8 us -> 0 us
  starting transfers between devices: 47.1 us -> 0 us
  local copies, waits for them, and re-layouts: 14.2 us -> 4.22 us
    pallas_call x2 -> x3, Pallas kernels: 46.6 us -> 110 us  [the longest x1 71.1 us: run_chain(): pl.pallas_call(functools.partial(chain_kernel, heads, n, n_outer), out_sh...]
    all_to_all x7 -> x0, waiting for transfers between devices: 58.8 us -> none  [the longest x5 46.1 us: inward(): return lax.all_to_all(x, 'inner', split_axis=1, concat_axis=0, tiled=True)]
    all_to_all x4 -> x0, blocking collectives: 51.8 us -> none  [the longest x3 44.5 us: outward(): return lax.all_to_all(x, 'inner', split_axis=0, concat_axis=1, tiled=True)]
    all_to_all x7 -> x0, starting transfers between devices: 47.1 us -> none  [the longest x5 32.3 us: inward(): return lax.all_to_all(x, 'inner', split_axis=1, concat_axis=0, tiled=True)]
    all_gather x2 -> x0, blocking collectives: 19.2 us -> none  [the longest x1 11 us: shards(): turned = lax.all_gather(first[0], 'outer', axis=0)]
    all_to_all x9 -> x0, local copies, waits for them, and re-layouts: 7.76 us -> none  [the longest x4 4.36 us: inward(): return lax.all_to_all(x, 'inner', split_axis=1, concat_axis=0, tiled=True)]
  transfers between devices with their start and end apart: 7 -> 0, of which waited for: 6 -> 0; matrix products, arithmetic and copies ran while one was open for 3% -> 0% of each run, Pallas kernels for 0% -> 0%
where the time goes in v2:
time: 116 us; the launch traced here: 115 us
  Pallas kernels  110 us (95%)
  local copies, waits for them, and re-layouts  4.22 us (4%)
    pallas_call x1, Pallas kernels, run_chain(): pl.pallas_call(functools.partial(chain_kernel, heads, n, n_outer), out_sh...  71.1 us
    pallas_call x1, Pallas kernels, run_first(): pl.pallas_call(functools.partial(first_kernel, count), grid=(heads // cou...  20.9 us
    pallas_call x1, Pallas kernels, run_final(): pl.pallas_call(functools.partial(final_kernel, count), grid=(heads // cou...  18.4 us

profile of v2, /device:TPU:25, one launch (start us, length us, event | category | flops | bytes accessed | tf_op | source)
XLA Modules:
  0.0 115.2 jit_solution(761704842355723985)
XLA Ops:
  0.6 0.0 copy-start.1
  0.6 1.4 %copy.14.b_ref = bf16[128,16]{1,0:T(8,128)(2,1)} copy(bf16[128,16]{0,1:T(8,128)(2,1)} %param.10) | data formatting | bytes 8192 | tf_op args[3]
  2.0 0.0 copy-done.1
  2.0 0.7 copy.15.g_ref
  2.8 20.9 %shard_map.110 = (f32[16,128,128]{2,1,0:T(8,128)}, f32[16,128,128]{2,1,0:T(8,128)}, f32[16,128,128]{2,1,0:T(8,128)}, f32[16,128,128]{2,1,0:T(8,128)}, f32[16,128...) custom-call(bf16[128,16]{1,0:T(8,128)(2,1)} %copy.14.b_ref, ...), custom_call_target="tpu_custom_call" | custom-call | tf_op jit(solution)/shard_map/pallas_call | solution.py:407
  23.7 71.1 %shard_map.111 = (f32[16,128,128]{2,1,0:T(8,128)}, f32[16,128,128]{2,1,0:T(8,128)}) custom-call(f32[2,128,128]{2,1,0:T(8,128)} %bitcast.1, f32[16,128,128]{2,1,0:T(8,128)} %get-tuple-element.19.m_ref, f32[16,128,128]{2,1,0:T(8,128)} %get-tuple-element.20.mt_ref, f32[16,128,128]{2,1,0:T(8,128)} %get-tuple-element.21.add_ref, ...), custom_call_target="tpu_custom_call" | custom-call | tf_op jit(solution)/shard_map/pallas_call | solution.py:424
  94.8 18.4 %shard_map.112 = (bf16[128,2048]{1,0:T(8,128)(2,1)}, bf16[128,2048]{1,0:T(8,128)(2,1)}, bf16[128,2048]{1,0:T(8,128)(2,1)}, bf16[128,16]{1,0:T(8,128)(2,1)}, bf16[128,16]{1,0:T(8,128)(2,1)}) custom-call(bf16[128,16]{1,0:T(8,128)(2,1)} %copy.14.b_ref, bf16[128,16]{1,0:T(8,128)(2,1)} %copy.15.g_ref, bf16[128,2048]{1,0:T(8,128)(2,1)} %q_ref.3, ...), custom_call_target="tpu_custom_call" | custom-call | tf_op jit(solution)/shard_map/pallas_call | solution.py:445
  113.1 0.0 copy-start
  113.1 1.4 %copy.16 = bf16[128,16]{0,1:T(8,128)(2,1)} copy(bf16[128,16]{1,0:T(8,128)(2,1)} %get-tuple-element.28) | data formatting | bytes 8192 | tf_op jit(solution)/shard_map/pallas_call | solution.py:445
  114.6 0.0 copy-done
  114.6 0.7 copy.17
Async XLA Ops:
  0.6 1.4 %copy-start.1 = (bf16[128,16]{0,1:T(8,128)(2,1)S(1)}, bf16[128,16]{0,1:T(8,128)(2,1)}, u32[]{:S(2)}) copy-start(bf16[128,16]{0,1:T(8,128)(2,1)} %param.11) | copy-start | bytes 12292
  113.1 1.4 %copy-start = (bf16[128,16]{1,0:T(8,128)(2,1)S(1)}, bf16[128,16]{1,0:T(8,128)(2,1)}, u32[]{:S(2)}) copy-start(bf16[128,16]{1,0:T(8,128)(2,1)} %get-tuple-element.29) | copy-start | bytes 12292

commit v3 on v2

v3 whole, which is shorter than its diff:
```python
import functools

import jax
import jax.numpy as jnp
from jax import lax
from jax.experimental import pallas as pl
from jax.experimental.pallas import tpu as pltpu
from jax.sharding import PartitionSpec as P

D = 128
C = 128
BF = jnp.bfloat16
F32 = jnp.float32
MESH = pl.DeviceIdType.MESH
VM = pl.BlockSpec(memory_space=pltpu.VMEM)
DIMS = {"nn": ((1,), (0,)), "nt": ((1,), (1,)), "tn": ((0,), (0,))}


def split(x):
    hi = x.astype(BF)
    return hi, (x - hi.astype(F32)).astype(BF)


def exact(x):
    return x.astype(BF), None


def dot(a, b, mode):
    return lax.dot_general(a, b, (DIMS[mode], ((), ())), preferred_element_type=F32)


def mm(a, b, mode):
    ka = 0 if mode == "tn" else 1
    kb = 1 if mode == "nt" else 0
    (ah, al), (bh, bl) = a, b
    if al is None and bl is None:
        return dot(ah, bh, mode)
    if al is None:
        return dot(jnp.concatenate([ah, ah], ka), jnp.concatenate([bh, bl], kb), mode)
    left = jnp.concatenate([ah, al], ka)
    if bl is None:
        return dot(left, jnp.concatenate([bh, bh], kb), mode)
    top = jnp.concatenate([bh, bl], 1 - kb)
    low = jnp.concatenate([bh, jnp.zeros_like(bl)], 1 - kb)
    both = dot(left, jnp.concatenate([top, low], kb), mode)
    n = both.shape[1] // 2
    return both[:, :n] + both[:, n:]


def iotas():
    return lax.broadcasted_iota(jnp.int32, (C, C), 0), lax.broadcasted_iota(jnp.int32, (C, C), 1)


def ones_where(mask):
    return jnp.where(mask, 1.0, 0.0).astype(BF)


def unit(x):
    r = lax.rsqrt(jnp.sum(x * x, axis=1, keepdims=True) + 1e-06)
    return x * r, r


def decays(gate, row, col):
    wide = gate
    rhs = jnp.concatenate([wide, jnp.where(row > col, wide, 0.0)], 1).astype(BF)
    both = dot(ones_where(row >= col), rhs, "nn")
    after = dot(ones_where(row < col), wide.astype(BF), "nn")
    pair = jnp.where(row >= col, jnp.exp(both[:, C:]), 0.0)
    return jnp.exp(both[:, :C]), jnp.exp(after), pair


def inverses(lowers, row, col):
    eye = jnp.where(row == col, 1.0, 0.0)
    done = [eye - jnp.where((row // 2 == col // 2), low, 0.0) for low in lowers]
    size = 2
    while size < C:
        pick = (row // (2 * size) == col // (2 * size)) & (row // size != col // size)
        halves = [split(t) for t in done]
        mids = [mm(t, split(jnp.where(pick, low, 0.0)), "nn") for t, low in zip(halves, lowers)]
        done = [t - mm(split(m), h, "nn") for t, m, h in zip(done, mids, halves)]
        size *= 2
    return done


def head_columns(b_ref, g_ref, h):
    heads = b_ref.shape[1]
    pick = ones_where(lax.broadcasted_iota(jnp.int32, (heads, C), 0) == h)
    return jax.nn.sigmoid(dot(b_ref[...], pick, "nn")), dot(g_ref[...], pick, "nn")


def grams(qn, kn, pair, row, col):
    qs, ks = split(qn), split(kn)
    left = (jnp.concatenate([qs[0], ks[0]], 0), jnp.concatenate([qs[1], ks[1]], 0))
    both = mm(left, ks, "nt")
    return both[:C] * pair, jnp.where(row > col, both[C:] * pair, 0.0)


def columns(h):
    return pl.ds(pl.multiple_of(h * D, D), D)


def group_stage(hs, args, keep):
    b_ref, g_ref, q_ref, k_ref, v_ref, c_ref = args
    row, col = iotas()
    eye = row == col
    data, lowers = [], []
    for h in hs:
        beta, gate = head_columns(b_ref, g_ref, h)
        growth, tail, pair = decays(gate, row, col)
        qn, _ = unit(q_ref[:, columns(h)].astype(F32))
        kn, _ = unit(k_ref[:, columns(h)].astype(F32))
        scores, gram = grams(qn, kn, pair, row, col)
        lowers.append(beta * gram)
        for name, value in (
            ("beta", beta), ("growth", growth), ("tail", tail),
            ("pair", pair), ("scores", scores), ("gram", gram),
        ):
            keep[name][h] = value
        cot = exact(c_ref[:, columns(h)])
        pc = mm(split(scores), cot, "tn")
        keep["pc"][h] = pc
        qpart = mm(split(qn * growth), cot, "tn")
        data.append((kn, beta, growth, tail, v_ref[:, columns(h)].astype(F32), pc, qpart))
    for h, inv, rest in zip(hs, inverses(lowers, row, col), data):
        kn, beta, growth, tail, val, pc, qpart = rest
        keep["inv"][h] = inv
        halves = split(inv)
        wk = mm(halves, split(beta * growth * kn), "nn")
        wv = mm(halves, split(beta * val), "nn")
        keep["wk"][h] = wk
        keep["wv"][h] = wv
        ws, ts = split(wk), split(kn * tail)
        last = jnp.where(eye, jnp.broadcast_to(growth[C - 1 :, :], (C, C)), 0.0)
        keep["m"][h] = last - mm(ts, ws, "tn")
        keep["mt"][h] = last - mm(ws, ts, "tn")
        keep["add"][h] = mm(ts, split(wv), "tn")
        keep["radd"][h] = qpart - mm(ws, split(pc), "tn")


def state_stage(hs, args, keep, dq_ref):
    _, _, q_ref, k_ref, _, c_ref = args
    for h in hs:
        qn, qr = unit(q_ref[:, columns(h)].astype(F32))
        kn, _ = unit(k_ref[:, columns(h)].astype(F32))
        cot = exact(c_ref[:, columns(h)])
        ss = split(keep["st"][h])
        new = keep["wv"][h] - mm(split(keep["wk"][h]), ss, "nn")
        ns = split(new)
        dsc = mm(cot, ns, "nt")
        dqg = keep["growth"][h] * mm(cot, ss, "nt")
        b1 = split(dsc * keep["pair"][h])
        dqn = mm(b1, split(kn), "nn") + dqg
        dq_ref[:, columns(h)] = (
            qr * (dqn - qn * jnp.sum(dqn * qn, axis=1, keepdims=True))
        ).astype(BF)
        keep["wv"][h] = new
        keep["wk"][h] = mm(b1, split(qn), "tn")
        keep["z"][h] = dsc * keep["scores"][h]
        keep["x"][h] = dqg * qn


def grad_stage(hs, args, keep, dk_ref, dv_ref, db_acc, dg_acc):
    _, _, _, k_ref, v_ref, _ = args
    row, col = iotas()
    upper = ones_where(row <= col)
    upper2 = jnp.concatenate([upper, upper], 1)
    lower = ones_where(row > col)
    lower2 = jnp.concatenate([lower, lower], 1)
    lane = lax.broadcasted_iota(jnp.int32, db_acc.shape, 1)
    for h in hs:
        kn, kr = unit(k_ref[:, columns(h)].astype(F32))
        val = v_ref[:, columns(h)].astype(F32)
        beta, growth, tail = keep["beta"][h], keep["growth"][h], keep["tail"][h]
        state = keep["st"][h]
        after = keep["bin"][h, :, :D] + mm(
            split(keep["bin"][h, :, D:]), split(keep["oin"][h]), "nn"
        )
        ss, fs, ns, ks = split(state), split(after), split(keep["wv"][h]), split(kn)
        tk = kn * tail
        dnew = keep["pc"][h] + mm(split(tk), fs, "nn")
        dtk = mm(ns, fs, "nt")
        err = mm(split(keep["inv"][h]), split(dnew), "tn")
        es = split(err)
        dkw = -mm(es, ss, "nt")
        dlow = jnp.where(row > col, -mm(es, ns, "nt"), 0.0)
        b2 = split(dlow * beta * keep["pair"][h])
        kgrow = growth * dkw
        dkn = (
            keep["wk"][h] + mm(b2, ks, "nn") + mm(b2, ks, "tn") + beta * kgrow + tail * dtk
        )
        dk_ref[:, columns(h)] = (
            kr * (dkn - kn * jnp.sum(dkn * kn, axis=1, keepdims=True))
        ).astype(BF)
        dv_ref[:, columns(h)] = (beta * err).astype(BF)
        kgrow = kn * kgrow
        dlg = dlow * keep["gram"][h]
        dbeta = jnp.sum((dlg + kgrow + err * val) * (beta * (1.0 - beta)), axis=1, keepdims=True)
        z = keep["z"][h] + beta * dlg
        x = keep["x"][h] + beta * kgrow
        zx = split(jnp.concatenate([z, x], 1))
        up = dot(upper2, jnp.concatenate(zx, 0), "nn")
        below = dot(lower2, jnp.concatenate(split(dtk * tk), 0), "nn")
        total = jnp.sum(
            jnp.sum(state * after * growth[C - 1 :, :], axis=1, keepdims=True),
            axis=0, keepdims=True,
        )
        dgate = total + jnp.sum(
            jnp.where(row > col, up[:, :C], 0.0) + up[:, C:] + below, axis=1, keepdims=True
        )
        db_acc[...] = jnp.where(lane == h, dbeta, db_acc[...])
        dg_acc[...] = jnp.where(lane == h, dgate, dg_acc[...])


KEPT = (
    "m", "mt", "add", "radd", "inv", "wk", "wv", "pc", "beta", "growth", "tail",
    "pair", "scores", "gram", "z", "x", "st", "sout", "oin", "oout",
)
QUAD, DUO = 4, 2


def chain_kernel(
    heads, n, n_outer,
    b_ref, g_ref, q_ref, k_ref, v_ref, c_ref, s0_ref,
    dq_ref, dk_ref, dv_ref, db_ref, dg_ref,
    *scratch,
):
    args = (b_ref, g_ref, q_ref, k_ref, v_ref, c_ref)
    keep = dict(zip(KEPT, scratch))
    bin_ref, bout, db_acc, dg_acc = scratch[len(KEPT) : len(KEPT) + 4]
    s0send, fsend, frecv, bsend, brecv, osend, orecv, rsend = scratch[len(KEPT) + 4 :]
    keep["bin"] = bin_ref
    m_ref, mt_ref, add_ref, radd_ref = (keep[x] for x in ("m", "mt", "add", "radd"))
    st_ref, sout, oin, oout = (keep[x] for x in ("st", "sout", "oin", "oout"))
    o, i = lax.axis_index("outer"), lax.axis_index("inner")
    hpd = s0_ref.shape[0]
    barrier = pltpu.get_barrier_semaphore()
    for d in range(1, n):
        pl.semaphore_signal(
            barrier, inc=1, device_id=(o, lax.rem(i + d, n)), device_id_type=MESH
        )
    for d in range(1, n_outer):
        pl.semaphore_signal(
            barrier, inc=1, device_id=(lax.rem(o + d, n_outer), i), device_id_type=MESH
        )
    pl.semaphore_wait(barrier, n + n_outer - 2)

    def remote(src, dst, send, recv, target):
        return pltpu.make_async_remote_copy(
            src_ref=src, dst_ref=dst, send_sem=send, recv_sem=recv,
            device_id=target, device_id_type=MESH,
        )

    def start_copy(j):
        h = i * hpd + j
        return remote(s0_ref.at[j], st_ref.at[h], s0send.at[j], frecv.at[h], (o, 0))

    def up_copy(h):
        return remote(sout.at[h], st_ref.at[h], fsend.at[h], frecv.at[h], (o, lax.rem(i + 1, n)))

    def down_copy(h):
        return remote(
            bout.at[h], bin_ref.at[h], bsend.at[h], brecv.at[h], (o, lax.rem(i + n - 1, n))
        )

    def outer_copy(h):
        return remote(
            oout.at[h], oin.at[h], osend.at[h], orecv.at[h],
            (lax.rem(o + n_outer - 1, n_outer), i),
        )

    def relay_copy(h, hop):
        return remote(
            oin.at[h], oin.at[h], rsend.at[h, hop - 1], orecv.at[h], (o, lax.rem(i + hop, n))
        )

    even = lax.rem(i, 2) == 0
    relays = o < n_outer - 1
    near = relays & even & (i + 1 < n)
    far = relays & even & (i + 2 < n)

    @pl.when(i == 0)
    def _():
        for j in range(hpd):
            pltpu.make_async_copy(s0_ref.at[j], st_ref.at[j], frecv.at[j]).start()

    @pl.when(i > 0)
    def _():
        for j in range(hpd):
            start_copy(j).start()

    lag_up = 2 * i
    lag_down = 2 * (n - 1 - i)
    lag_outer = 2 * (n - 1) + 2 * (n_outer - 1 - o)
    lag_in = lag_outer + 2 * (i // 2 + lax.rem(i, 2))
    lag_state = jnp.maximum(heads, lag_up + DUO - 1)
    lag_grad = jnp.maximum(lag_in + DUO - 1, lag_state + 1)
    db_acc[...] = jnp.zeros_like(db_acc)
    dg_acc[...] = jnp.zeros_like(dg_acc)

    @pl.when(o == n_outer - 1)
    def _():
        oin[...] = jnp.zeros_like(oin)

    def tick(t, carry):
        @pl.when((lax.rem(t, QUAD) == 0) & (t < heads))
        def _():
            group_stage([t + s for s in range(QUAD)], args, keep)

        up = t - lag_up

        @pl.when((up >= 0) & (up < heads))
        def _():
            pltpu.make_async_copy(st_ref.at[up], st_ref.at[up], frecv.at[up]).wait()

            @pl.when(i < n - 1)
            def _():
                sout[up] = mm(split(m_ref[up]), split(st_ref[up]), "nn") + add_ref[up]
                up_copy(up).start()

        down = t - lag_down

        @pl.when((down >= 0) & (down < heads))
        def _():
            @pl.when(i == n - 1)
            def _():
                row, col = iotas()
                bin_ref[down, :, :D] = jnp.zeros((D, D), F32)
                bin_ref[down, :, D:] = jnp.where(row == col, 1.0, 0.0)
                bout[down, :, :D] = radd_ref[down]
                bout[down, :, D:] = mt_ref[down]

            @pl.when(i < n - 1)
            def _():
                down_copy(down).wait_recv()
                turned = split(mt_ref[down])
                bout[down, :, :D] = (
                    mm(turned, split(bin_ref[down, :, :D]), "nn") + radd_ref[down]
                )
                bout[down, :, D:] = mm(turned, split(bin_ref[down, :, D:]), "nn")

            @pl.when(i > 0)
            def _():
                down_copy(down).start()

        last = t - lag_in

        @pl.when((last >= 0) & (last < heads))
        def _():
            @pl.when(relays)
            def _():
                outer_copy(last).wait_recv()

            @pl.when(near)
            def _():
                relay_copy(last, 1).start()

            @pl.when(far)
            def _():
                relay_copy(last, 2).start()

            @pl.when((i == 0) & (o > 0) & relays)
            def _():
                oout[last] = (
                    mm(split(bout[last, :, D:]), split(oin[last]), "nn") + bout[last, :, :D]
                )

            @pl.when((i == 0) & (o > 0) & (o == n_outer - 1))
            def _():
                oout[last] = bout[last, :, :D]

            @pl.when((i == 0) & (o > 0))
            def _():
                outer_copy(last).start()

        first = t - lag_state

        @pl.when((first >= 0) & (first < heads) & (lax.rem(first, DUO) == 0))
        def _():
            state_stage([first + s for s in range(DUO)], args, keep, dq_ref)

        done = t - lag_grad

        @pl.when((done >= 0) & (done < heads) & (lax.rem(done, DUO) == 0))
        def _():
            grad_stage([done + s for s in range(DUO)], args, keep, dk_ref, dv_ref, db_acc, dg_acc)

        return carry

    lax.fori_loop(0, lag_grad + heads, tick, 0)
    db_ref[...] = db_acc[...].astype(BF)
    dg_ref[...] = dg_acc[...].astype(BF)

    @pl.when(i > 0)
    def _():
        for j in range(hpd):
            start_copy(j).wait_send()

    def finish(h, carry):
        @pl.when(i < n - 1)
        def _():
            up_copy(h).wait_send()

        @pl.when(i > 0)
        def _():
            down_copy(h).wait_send()

        @pl.when((i == 0) & (o > 0))
        def _():
            outer_copy(h).wait_send()

        @pl.when(near)
        def _():
            relay_copy(h, 1).wait_send()

        @pl.when(far)
        def _():
            relay_copy(h, 2).wait_send()

        return carry

    lax.fori_loop(0, heads, finish, 0)


def shards(n, n_outer, queries, key_rows, value_rows, beta_logit, log_gate, out_grad, block_states):
    heads = beta_logit.shape[1]
    big = jax.ShapeDtypeStruct(queries.shape, BF)
    thin = jax.ShapeDtypeStruct(beta_logit.shape, BF)
    one = pltpu.VMEM((heads, D, D), F32)
    two = pltpu.VMEM((heads, D, 2 * D), F32)
    acc = pltpu.VMEM((C, heads), F32)
    sems = pltpu.SemaphoreType.DMA((heads,))
    return pl.pallas_call(
        functools.partial(chain_kernel, heads, n, n_outer),
        out_shape=(big, big, big, thin, thin),
        in_specs=[VM] * 7,
        out_specs=(VM,) * 5,
        scratch_shapes=[one] * len(KEPT) + [two, two, acc, acc] + [
            pltpu.SemaphoreType.DMA((block_states.shape[1],)), sems, sems, sems, sems, sems, sems,
            pltpu.SemaphoreType.DMA((heads, 2)),
        ],
        compiler_params=pltpu.CompilerParams(
            vmem_limit_bytes=56 << 20, collective_id=0, has_side_effects=True
        ),
    )(beta_logit, log_gate, queries, key_rows, value_rows, out_grad, block_states[0])


def solution(mesh):
    wide = P(("outer", "inner"), None)
    return jax.shard_map(
        functools.partial(shards, mesh.shape["inner"], mesh.shape["outer"]),
        mesh=mesh,
        in_specs=(wide,) * 6 + (P("outer", "inner", None, None),),
        out_specs=(wide,) * 5,
        check_vma=False,
    )
```

time: 116 us -> 92.4 us (0.80)
  Pallas kernels: 110 us -> 83.2 us
  local copies, waits for them, and re-layouts: 4.22 us -> 8.2 us
    pallas_call x3 -> x1, Pallas kernels: 110 us -> 83.2 us  [shards(): pl.pallas_call(functools.partial(chain_kernel, heads, n, n_outer), out_sh...]
    unnamed x6 -> x13, local copies, waits for them, and re-layouts: 2.12 us -> 6.1 us
where the time goes in v3:
time: 92.4 us; the launch traced here: 92.1 us
  Pallas kernels  83.2 us (90%)
  local copies, waits for them, and re-layouts  8.2 us (9%)
    pallas_call x1, Pallas kernels, shards(): pl.pallas_call(functools.partial(chain_kernel, heads, n, n_outer), out_sh...  83.2 us
    unnamed x13, local copies, waits for them, and re-layouts  6.1 us
    pallas_call x2, local copies, waits for them, and re-layouts, shards(): pl.pallas_call(functools.partial(chain_kernel, heads, n, n_outer), out_sh...  2.1 us

profile of v3, /device:TPU:25, one launch (start us, length us, event | category | flops | bytes accessed | tf_op | source)
XLA Modules:
  0.0 92.1 jit_solution(6093276452008227831)
XLA Ops:
  0.6 0.0 copy-start.3
  0.6 1.4 %copy.12.b_ref = bf16[128,16]{1,0:T(8,128)(2,1)} copy(bf16[128,16]{0,1:T(8,128)(2,1)} %param.10) | data formatting | bytes 8192 | tf_op args[3]
  2.0 0.0 copy-done.3
  2.1 0.7 copy.13.g_ref
  2.8 83.2 %shard_map.110 = (bf16[128,2048]{1,0:T(8,128)(2,1)}, bf16[128,2048]{1,0:T(8,128)(2,1)}, bf16[128,2048]{1,0:T(8,128)(2,1)}, bf16[128,16]{1,0:T(8,128)(2,1)}, bf16[128,16]{1,0:T(8,128)(2,1)}) custom-call(bf16[128,16]{1,0:T(8,128)(2,1)} %copy.12.b_ref, bf16[128,16]{1,0:T(8,128)(2,1)} %copy.13.g_ref, bf16[128,2048]{1,0:T(8,128)(2,1)} %q_ref.1, ...), custom_call_target="tpu_custom_call" | custom-call | tf_op jit(solution)/shard_map/pallas_call | solution.py:432
  86.0 0.0 copy-start.2
  86.0 1.4 %copy.14 = bf16[128,16]{0,1:T(8,128)(2,1)} copy(bf16[128,16]{1,0:T(8,128)(2,1)} %get-tuple-element.8) | data formatting | bytes 8192 | tf_op jit(solution)/shard_map/pallas_call | solution.py:432
  87.4 0.0 copy-done.2
  87.4 0.7 copy.15
  88.1 0.0 copy-start.1
  88.1 1.9 %copy.19 = bf16[128,2048]{1,0:T(8,128)(2,1)} copy(bf16[128,2048]{1,0:T(8,128)(2,1)} %get-tuple-element.15) | data formatting | bytes 1048576
  90.0 0.0 copy-done.1
  90.0 0.0 copy-start
  90.0 0.8 copy.20
  90.8 0.4 copy-done
  91.3 0.8 copy.21
Async XLA Ops:
  0.6 1.4 %copy-start.3 = (bf16[128,16]{0,1:T(8,128)(2,1)S(1)}, bf16[128,16]{0,1:T(8,128)(2,1)}, u32[]{:S(2)}) copy-start(bf16[128,16]{0,1:T(8,128)(2,1)} %param.11) | copy-start | bytes 12292
  86.0 1.4 %copy-start.2 = (bf16[128,16]{1,0:T(8,128)(2,1)S(1)}, bf16[128,16]{1,0:T(8,128)(2,1)}, u32[]{:S(2)}) copy-start(bf16[128,16]{1,0:T(8,128)(2,1)} %get-tuple-element.9) | copy-start | bytes 12292
  88.1 1.9 %copy-start.1 = (bf16[128,2048]{1,0:T(8,128)(2,1)S(1)}, bf16[128,2048]{1,0:T(8,128)(2,1)}, u32[]{:S(2)}) copy-start(bf16[128,2048]{1,0:T(8,128)(2,1)} %get-tuple-element.16) | copy-start | bytes 1572868
  90.0 1.2 %copy-start = (bf16[128,2048]{1,0:T(8,128)(2,1)S(1)}, bf16[128,2048]{1,0:T(8,128)(2,1)}, u32[]{:S(2)}) copy-start(bf16[128,2048]{1,0:T(8,128)(2,1)} %get-tuple-element.17) | copy-start | bytes 1572868

commit v4 on v3

--- a/solution.py
+++ b/solution.py
@@ -83,9 +83,9 @@
 
 
 def head_columns(b_ref, g_ref, h):
-    heads = b_ref.shape[1]
+    heads = b_ref.shape[0]
     pick = ones_where(lax.broadcasted_iota(jnp.int32, (heads, C), 0) == h)
-    return jax.nn.sigmoid(dot(b_ref[...], pick, "nn")), dot(g_ref[...], pick, "nn")
+    return jax.nn.sigmoid(dot(b_ref[...], pick, "tn")), dot(g_ref[...], pick, "tn")
 
 
 def grams(qn, kn, pair, row, col):
@@ -131,8 +131,8 @@
         keep["wv"][h] = wv
         ws, ts = split(wk), split(kn * tail)
         last = jnp.where(eye, jnp.broadcast_to(growth[C - 1 :, :], (C, C)), 0.0)
-        keep["m"][h] = last - mm(ts, ws, "tn")
-        keep["mt"][h] = last - mm(ws, ts, "tn")
+        keep["m"][h] = jnp.concatenate(split(last - mm(ts, ws, "tn")), 1)
+        keep["mt"][h] = jnp.concatenate(split(last - mm(ws, ts, "tn")), 1)
         keep["add"][h] = mm(ts, split(wv), "tn")
         keep["radd"][h] = qpart - mm(ws, split(pc), "tn")
 
@@ -212,10 +212,14 @@
 
 
 KEPT = (
-    "m", "mt", "add", "radd", "inv", "wk", "wv", "pc", "beta", "growth", "tail",
+    "add", "radd", "inv", "wk", "wv", "pc", "beta", "growth", "tail",
     "pair", "scores", "gram", "z", "x", "st", "sout", "oin", "oout",
 )
 QUAD, DUO = 4, 2
+
+
+def pair_of(ref, h):
+    return ref[h, :, :D], ref[h, :, D:]
 
 
 def chain_kernel(
@@ -226,10 +230,10 @@
 ):
     args = (b_ref, g_ref, q_ref, k_ref, v_ref, c_ref)
     keep = dict(zip(KEPT, scratch))
-    bin_ref, bout, db_acc, dg_acc = scratch[len(KEPT) : len(KEPT) + 4]
-    s0send, fsend, frecv, bsend, brecv, osend, orecv, rsend = scratch[len(KEPT) + 4 :]
-    keep["bin"] = bin_ref
-    m_ref, mt_ref, add_ref, radd_ref = (keep[x] for x in ("m", "mt", "add", "radd"))
+    bin_ref, bout, m_ref, mt_ref, db_acc, dg_acc = scratch[len(KEPT) : len(KEPT) + 6]
+    s0send, fsend, frecv, bsend, brecv, osend, orecv, rsend = scratch[len(KEPT) + 6 :]
+    keep["bin"], keep["m"], keep["mt"] = bin_ref, m_ref, mt_ref
+    add_ref, radd_ref = keep["add"], keep["radd"]
     st_ref, sout, oin, oout = (keep[x] for x in ("st", "sout", "oin", "oout"))
     o, i = lax.axis_index("outer"), lax.axis_index("inner")
     hpd = s0_ref.shape[0]
@@ -301,46 +305,46 @@
     def _():
         oin[...] = jnp.zeros_like(oin)
 
+    @pl.when(i == n - 1)
+    def _():
+        row, col = iotas()
+        ident = jnp.where(row == col, 1.0, 0.0)
+        for h in range(heads):
+            bin_ref[h] = jnp.concatenate([jnp.zeros_like(ident), ident], 1)
+
     def tick(t, carry):
         @pl.when((lax.rem(t, QUAD) == 0) & (t < heads))
         def _():
             group_stage([t + s for s in range(QUAD)], args, keep)
 
-        up = t - lag_up
-
-        @pl.when((up >= 0) & (up < heads))
+        up, down = t - lag_up, t - lag_down
+        up_ok = (up >= 0) & (up < heads)
+        down_ok = (down >= 0) & (down < heads)
+
+        @pl.when(up_ok)
         def _():
             pltpu.make_async_copy(st_ref.at[up], st_ref.at[up], frecv.at[up]).wait()
 
-            @pl.when(i < n - 1)
-            def _():
-                sout[up] = mm(split(m_ref[up]), split(st_ref[up]), "nn") + add_ref[up]
-                up_copy(up).start()
-
-        down = t - lag_down
-
-        @pl.when((down >= 0) & (down < heads))
-        def _():
-            @pl.when(i == n - 1)
-            def _():
-                row, col = iotas()
-                bin_ref[down, :, :D] = jnp.zeros((D, D), F32)
-                bin_ref[down, :, D:] = jnp.where(row == col, 1.0, 0.0)
-                bout[down, :, :D] = radd_ref[down]
-                bout[down, :, D:] = mt_ref[down]
-
-            @pl.when(i < n - 1)
-            def _():
-                down_copy(down).wait_recv()
-                turned = split(mt_ref[down])
-                bout[down, :, :D] = (
-                    mm(turned, split(bin_ref[down, :, :D]), "nn") + radd_ref[down]
-                )
-                bout[down, :, D:] = mm(turned, split(bin_ref[down, :, D:]), "nn")
-
-            @pl.when(i > 0)
-            def _():
-                down_copy(down).start()
+        @pl.when(down_ok & (i < n - 1))
+        def _():
+            down_copy(down).wait_recv()
+
+        @pl.when(up_ok | down_ok)
+        def _():
+            at_up, at_down = jnp.where(up_ok, up, heads), jnp.where(down_ok, down, heads)
+            moved = mm(pair_of(m_ref, at_up), split(st_ref[at_up]), "nn") + add_ref[at_up]
+            back = mm(pair_of(mt_ref, at_down), split(bin_ref[at_down]), "nn")
+            grad = back[:, :D] + radd_ref[at_down]
+            sout[at_up] = moved
+            bout[at_down] = jnp.concatenate([grad, back[:, D:]], 1)
+
+        @pl.when(up_ok & (i < n - 1))
+        def _():
+            up_copy(up).start()
+
+        @pl.when(down_ok & (i > 0))
+        def _():
+            down_copy(down).start()
 
         last = t - lag_in
 
@@ -358,16 +362,12 @@
             def _():
                 relay_copy(last, 2).start()
 
-            @pl.when((i == 0) & (o > 0) & relays)
+            @pl.when((i == 0) & (o > 0))
             def _():
                 oout[last] = (
                     mm(split(bout[last, :, D:]), split(oin[last]), "nn") + bout[last, :, :D]
                 )
 
-            @pl.when((i == 0) & (o > 0) & (o == n_outer - 1))
-            def _():
-                oout[last] = bout[last, :, :D]
-
             @pl.when((i == 0) & (o > 0))
             def _():
                 outer_copy(last).start()
@@ -387,8 +387,8 @@
         return carry
 
     lax.fori_loop(0, lag_grad + heads, tick, 0)
-    db_ref[...] = db_acc[...].astype(BF)
-    dg_ref[...] = dg_acc[...].astype(BF)
+    db_ref[...] = db_acc[...].T[:heads].astype(BF)
+    dg_ref[...] = dg_acc[...].T[:heads].astype(BF)
 
     @pl.when(i > 0)
     def _():
@@ -424,24 +424,26 @@
 def shards(n, n_outer, queries, key_rows, value_rows, beta_logit, log_gate, out_grad, block_states):
     heads = beta_logit.shape[1]
     big = jax.ShapeDtypeStruct(queries.shape, BF)
-    thin = jax.ShapeDtypeStruct(beta_logit.shape, BF)
-    one = pltpu.VMEM((heads, D, D), F32)
-    two = pltpu.VMEM((heads, D, 2 * D), F32)
-    acc = pltpu.VMEM((C, heads), F32)
+    thin = jax.ShapeDtypeStruct((heads, C), BF)
+    one = pltpu.VMEM((heads + 1, D, D), F32)
+    two = pltpu.VMEM((heads + 1, D, 2 * D), F32)
+    halves = pltpu.VMEM((heads + 1, D, 2 * D), BF)
+    acc = pltpu.VMEM((C, D), F32)
     sems = pltpu.SemaphoreType.DMA((heads,))
-    return pl.pallas_call(
+    dq, dk, dv, db, dg = pl.pallas_call(
         functools.partial(chain_kernel, heads, n, n_outer),
         out_shape=(big, big, big, thin, thin),
         in_specs=[VM] * 7,
         out_specs=(VM,) * 5,
-        scratch_shapes=[one] * len(KEPT) + [two, two, acc, acc] + [
+        scratch_shapes=[one] * len(KEPT) + [two, two, halves, halves, acc, acc] + [
             pltpu.SemaphoreType.DMA((block_states.shape[1],)), sems, sems, sems, sems, sems, sems,
             pltpu.SemaphoreType.DMA((heads, 2)),
         ],
         compiler_params=pltpu.CompilerParams(
             vmem_limit_bytes=56 << 20, collective_id=0, has_side_effects=True
         ),
-    )(beta_logit, log_gate, queries, key_rows, value_rows, out_grad, block_states[0])
+    )(beta_logit.T, log_gate.T, queries, key_rows, value_rows, out_grad, block_states[0])
+    return dq, dk, dv, db.T, dg.T
 
 
 def solution(mesh):

time: 92.4 us -> 90.5 us (0.979)
  local copies, waits for them, and re-layouts: 8.2 us -> 5.24 us
  Pallas kernels: 83.2 us -> 84.3 us
    pallas_call x2 -> x0, local copies, waits for them, and re-layouts: 2.1 us -> none  [shards(): pl.pallas_call(functools.partial(chain_kernel, heads, n, n_outer), out_sh...]
    pallas_call x1, Pallas kernels: 83.2 us -> 84.3 us  [shards(): pl.pallas_call(functools.partial(chain_kernel, heads, n, n_outer), out_sh...]
where the time goes in v4:
time: 90.5 us; the launch traced here: 90.2 us
  Pallas kernels  84.3 us (93%)
  local copies, waits for them, and re-layouts  5.24 us (6%)
    pallas_call x1, Pallas kernels, shards(): pl.pallas_call(functools.partial(chain_kernel, heads, n, n_outer), out_sh...  84.3 us
    unnamed x13, local copies, waits for them, and re-layouts  5.24 us

profile of v4, /device:TPU:25, one launch (start us, length us, event | category | flops | bytes accessed | tf_op | source)
XLA Modules:
  0.0 90.2 jit_solution(7062474001983016747)
XLA Ops:
  0.6 84.3 %shard_map.110 = (bf16[128,2048]{1,0:T(8,128)(2,1)}, bf16[128,2048]{1,0:T(8,128)(2,1)}, bf16[128,2048]{1,0:T(8,128)(2,1)}, bf16[16,128]{1,0:T(8,128)(2,1)}, bf16[16,128]{1,0:T(8,128)(2,1)}) custom-call(bf16[16,128]{1,0:T(8,128)(2,1)} %bitcast.6, bf16[16,128]{1,0:T(8,128)(2,1)} %bitcast.7, bf16[128,2048]{1,0:T(8,128)(2,1)} %q_ref.1, bf16[128,2048]{1,0:T(8,128)(2,1)} %k_ref.1, ...), custom_call_target="tpu_custom_call" | custom-call | tf_op jit(solution)/shard_map/pallas_call | solution.py:433
  85.0 0.0 copy-start.1
  85.0 1.9 %copy.17 = bf16[128,2048]{1,0:T(8,128)(2,1)} copy(bf16[128,2048]{1,0:T(8,128)(2,1)} %get-tuple-element.20) | data formatting | bytes 1048576
  86.9 0.0 copy-done.1
  86.9 0.0 copy-start
  86.9 0.8 copy.18
  87.7 0.4 copy-done
  88.1 0.0 copy-start.3
  88.1 0.8 copy.19
  88.9 0.0 copy-done.3
  88.9 0.0 copy-start.2
  88.9 0.6 copy.20
  89.5 0.1 copy-done.2
  89.6 0.6 copy.21
Async XLA Ops:
  85.0 2.0 %copy-start.1 = (bf16[128,2048]{1,0:T(8,128)(2,1)S(1)}, bf16[128,2048]{1,0:T(8,128)(2,1)}, u32[]{:S(2)}) copy-start(bf16[128,2048]{1,0:T(8,128)(2,1)} %get-tuple-element.21) | copy-start | bytes 1572868
  86.9 1.2 %copy-start = (bf16[128,2048]{1,0:T(8,128)(2,1)S(1)}, bf16[128,2048]{1,0:T(8,128)(2,1)}, u32[]{:S(2)}) copy-start(bf16[128,2048]{1,0:T(8,128)(2,1)} %get-tuple-element.22) | copy-start | bytes 1572868
  88.1 0.8 copy-start.3
  88.9 0.7 copy-start.2
